TPU v7x, 32 devices: a whole 2x2x4 slice. The times are simulated.
32 devices in a mesh: row: 16 (over z, x, core), col: 2 (over y).
Axes of the slice: x: 2, y: 2, z: 4, core: 2. Of those that a mesh axis runs over, the one named last changes fastest.
Arguments:
- forcing: float32 [16, 2, 96, 2048], P('row', 'col'), may hold values from -4 to 4
- local_op: bfloat16 [16, 2, 2048, 2048], P('row', 'col'), may hold values from -0.027621359 to 1.0376214
- material: int32 [16, 2, 2048], P('row', 'col'), may hold values from 0 to 7
- stiffness: float32 [8], replicated, may hold values from 0.25 to 4
Outputs:
- preconditioned: float32 [16, 2, 96, 2048], P('row', 'col')
- residual: float32 [16, 2, 96, 2048], P('row', 'col')
All inputs are finite; a program needn't handle non-finite values.
Results may differ from a plain program's by a relative error of at most 0.007.
Values may be sent and summed in bfloat16 or wider, within the bound.
A program may use at most 64 MiB of HBM per device.

v0:
```python
import jax
import jax.numpy as jnp
from jax import lax
from jax.sharding import PartitionSpec as P

HEADINGS = ((1, 1), (1, -1), (-1, 1), (-1, -1))


def shortened(array):

    def short(part):
        return part.astype(jnp.bfloat16) if part.dtype == jnp.float32 else part

    return jax.tree.map(short, array)


def padded(block, sides, width):
    for axis, dim in sides:
        count = lax.axis_size(axis)
        forward = [(i, i + 1) for i in range(count - 1)]
        backward = [(target, source) for source, target in forward]
        low = lax.ppermute(
            lax.slice_in_dim(block, block.shape[dim] - width, None, axis=dim), axis, forward
        )
        high = lax.ppermute(lax.slice_in_dim(block, 0, width, axis=dim), axis, backward)
        block = jnp.concatenate([low, block, high], axis=dim)
    return block


def exchange_faces(row_pair, col_pair):
    row_ext = padded(shortened(row_pair), (("row", 0),), 1).astype(row_pair.dtype)
    col_ext = padded(shortened(col_pair), (("col", 0),), 1).astype(col_pair.dtype)
    return (row_ext[0], row_ext[3], col_ext[0], col_ext[3])


def side_of(values, side_index):
    side_width = values.shape[-1] // 4
    return values[:, side_index * side_width : (side_index + 1) * side_width]


def sides_for(heading_index):
    in_row, out_row = (0, 1) if HEADINGS[heading_index][0] > 0 else (1, 0)
    in_col, out_col = (2, 3) if HEADINGS[heading_index][1] > 0 else (3, 2)
    return (in_row, out_row, in_col, out_col)


def local(forcing, local_op, material, stiffness):
    source = forcing[0, 0]
    matrix = local_op[0, 0]
    load_count, order_size = source.shape
    side_width = order_size // 4
    row_count = lax.axis_size("row")
    col_count = lax.axis_size("col")
    row_place = lax.axis_index("row")
    col_place = lax.axis_index("col")
    forcing_half = source.astype(jnp.bfloat16)
    arrival_ticks = []
    for heading in HEADINGS:
        row_part = row_place if heading[0] > 0 else row_count - 1 - row_place
        col_part = col_place if heading[1] > 0 else col_count - 1 - col_place
        arrival_ticks.append(row_part + col_part)
    zero_trace = jnp.zeros((load_count, side_width), jnp.bfloat16)
    base = jnp.dot(forcing_half, matrix, preferred_element_type=jnp.float32)

    def rows_of(side_index):
        return matrix[side_index * side_width : (side_index + 1) * side_width]

    def block_of(row_side, col_side):
        return matrix[
            row_side * side_width : (row_side + 1) * side_width,
            col_side * side_width : (col_side + 1) * side_width,
        ]

    def solve_sides(heading_index, row_trace, col_trace):
        in_row, out_row, in_col, out_col = sides_for(heading_index)
        outputs = []
        for out_side in (out_row, out_col):
            value = side_of(base, out_side)
            value = value + jnp.dot(
                row_trace, block_of(in_row, out_side), preferred_element_type=jnp.float32
            )
            value = value + jnp.dot(
                col_trace, block_of(in_col, out_side), preferred_element_type=jnp.float32
            )
            outputs.append(value.astype(jnp.bfloat16))
        return (outputs[0], outputs[1])

    def tick_step(tick_number, state_now):
        row_traces, col_traces, summed, kept_rows, kept_cols = state_now
        out_rows = []
        out_cols = []
        kept_rows = list(kept_rows)
        kept_cols = list(kept_cols)
        for heading_index in range(4):
            active = tick_number == arrival_ticks[heading_index]

            def working(operands, heading_index=heading_index):
                return solve_sides(heading_index, operands[0], operands[1])

            def resting(operands):
                return (zero_trace, zero_trace)

            row_out, col_out = lax.cond(
                active, working, resting, (row_traces[heading_index], col_traces[heading_index])
            )
            kept_rows[heading_index] = jnp.where(
                active, row_traces[heading_index], kept_rows[heading_index]
            )
            kept_cols[heading_index] = jnp.where(
                active, col_traces[heading_index], kept_cols[heading_index]
            )
            out_rows.append(row_out)
            out_cols.append(col_out)
        row_pair = jnp.stack([out_rows[2] + out_rows[3], out_rows[0] + out_rows[1]])
        col_pair = jnp.stack([out_cols[1] + out_cols[3], out_cols[0] + out_cols[2]])
        from_above, from_below, from_left, from_right = exchange_faces(row_pair, col_pair)
        row_traces = (from_above, from_above, from_below, from_below)
        col_traces = (from_left, from_right, from_left, from_right)
        return (row_traces, col_traces, summed, tuple(kept_rows), tuple(kept_cols))

    tick_count = row_count + col_count - 1
    start_state = (
        (zero_trace,) * 4,
        (zero_trace,) * 4,
        jnp.zeros((load_count, order_size), jnp.float32),
        (zero_trace,) * 4,
        (zero_trace,) * 4,
    )
    row_traces, col_traces, summed, kept_rows, kept_cols = lax.fori_loop(
        0, tick_count, tick_step, start_state
    )
    summed = 4.0 * base
    for heading_index in range(4):
        in_row, out_row, in_col, out_col = sides_for(heading_index)
        summed = summed + jnp.dot(
            kept_rows[heading_index], rows_of(in_row), preferred_element_type=jnp.float32
        )
        summed = summed + jnp.dot(
            kept_cols[heading_index], rows_of(in_col), preferred_element_type=jnp.float32
        )
    preconditioned = summed * 0.25
    rounded = preconditioned.astype(jnp.bfloat16)
    row_pair = jnp.stack([side_of(rounded, 0), side_of(rounded, 1)])[:, None]
    col_pair = jnp.stack([side_of(rounded, 2), side_of(rounded, 3)])[:, None]
    from_above, from_below, from_left, from_right = exchange_faces(row_pair, col_pair)
    facing = jnp.concatenate(
        [from_above[0], from_below[0], from_left[0], from_right[0]], axis=1
    ).astype(jnp.float32)
    classes = jnp.arange(stiffness.shape[0], dtype=jnp.int32)
    coupling = jnp.sum(
        jnp.where(material[0, 0][None, :] == classes[:, None], stiffness[:, None], 0.0), axis=0
    )
    residual = source - preconditioned + coupling[None, :] * (facing - preconditioned)
    return (preconditioned[None, None], residual[None, None])


def solution(mesh):
    return jax.shard_map(
        local,
        mesh=mesh,
        in_specs=(
            P("row", "col", None, None),
            P("row", "col", None, None),
            P("row", "col", None),
            P(),
        ),
        out_specs=(P("row", "col", None, None), P("row", "col", None, None)),
        check_vma=False,
    )
```

profile of v0, /device:TPU:0, one launch (start us, length us, event | category | flops | bytes accessed | tf_op | source)
XLA Modules:
  0.0 342.3 jit_solution(4194190201231528074)
XLA Ops:
  0.7 5.1 %fusion.43 = f32[96,2048]{1,0:T(8,128)S(1)} fusion(f32[1,1,96,2048]{3,2,1,0:T(8,128)} %param.14, bf16[1,1,2048,2048]{3,2,1,0:T(8,128)(2,1)} %param.15), kind=kOutput, calls=%fused_computation.80 | convolution fusion | flops 805502976 | bytes 9961472 | tf_op jit(solution)/shard_map/dot_general | solution.py:63
  6.0 313.8 %while.44 = (s32[]{:T(128)}, bf16[96,512]{1,0:T(8,128)(2,1)S(1)}, bf16[96,512]{1,0:T(8,128)(2,1)S(1)}, bf16[96,512]{1,0:T(8,128)(2,1)S(1)}, bf16[96,512]{1,0:T(8...) while((s32[]{:T(128)}, bf16[96,512]{1,0:T(8,128)(2,1)S(1)}, ...), condition=%wide.region_9.10_spmd.clone, body=%wide.region_0.9_spmd.clone.sunk | while | flops 807469056 | bytes 22151820 | solution.py:129
  6.0 5.1 %conditional.12 = (bf16[96,512]{1,0:T(8,128)(2,1)S(1)}, bf16[96,512]{1,0:T(8,128)(2,1)S(1)}) conditional(s32[]{:T(128)} %convert_element_type.90, () %tuple.100, (f32[96,2048]{1,0:T(8,128)S(1)}, bf16[2048,2048]{1,0:T(8,128)(2,1)}, bf16[96,512]{1,0:T(8,128)(2,1)S(1)}, bf16[96,512]{1,0:T(8,128)(2,1)S(1)}) %tuple.101), branch_computations={%region_1.0_spmd, %region_2.0_spmd} | conditional | flops 201621504 | bytes 3866640 | solution.py:103
  13.9 4.9 %collective-permute-start.2 = (bf16[1,96,512]{2,1,0:T(8,128)(2,1)S(1)}, bf16[1,96,512]{2,1,0:T(8,128)(2,1)S(1)}, u32[]{:S(2)}, u32[]{:S(2)}) collective-permute-start(bf16[1,96,512]{2,1,0:T(8,128)(2,1)S(1)} %add_bitcast_fusion.10), channel_id=1, source_target_pairs={{0,1},{2,3},{4,5},{6,7},{8,9},{10,11},{12,13},{14,15},{16,17},{18,... | collective-permute-start | bytes 294920 | tf_op jit(solution)/shard_map/while/body/eval_jaxpr/ppermute | solution.py:22
  21.8 4.4 %collective-permute-done.3 = bf16[1,96,512]{2,1,0:T(8,128)(2,1)S(1)} collective-permute-done((bf16[1,96,512]{2,1,0:T(8,128)(2,1)S(1)}, bf16[1,96,512]{2,1,0:T(8,128)(2,1)S(1)}, u32[]{:S(2)}, u32[]{:S(2)}) %collective-permute-start.3) | collective-permute-done | bytes 98336 | tf_op jit(solution)/shard_map/while/body/eval_jaxpr/ppermute | solution.py:25
  26.4 5.1 %conditional.13 = (bf16[96,512]{1,0:T(8,128)(2,1)S(1)}, bf16[96,512]{1,0:T(8,128)(2,1)S(1)}) conditional(s32[]{:T(128)} %convert_element_type.91, () %tuple.102, (f32[96,2048]{1,0:T(8,128)S(1)}, bf16[2048,2048]{1,0:T(8,128)(2,1)}, bf16[96,512]{1,0:T(8,128)(2,1)S(1)}, bf16[96,512]{1,0:T(8,128)(2,1)S(1)}) %tuple.103), branch_computations={%region_3.3_spmd, %region_4.4_spmd} | conditional | flops 201621504 | bytes 3866640 | solution.py:103
  31.5 1.9 collective-permute-start
  39.2 4.7 %collective-permute-done.3 = bf16[1,96,512]{2,1,0:T(8,128)(2,1)S(1)} collective-permute-done((bf16[1,96,512]{2,1,0:T(8,128)(2,1)S(1)}, bf16[1,96,512]{2,1,0:T(8,128)(2,1)S(1)}, u32[]{:S(2)}, u32[]{:S(2)}) %collective-permute-start.3) | collective-permute-done | bytes 98336 | tf_op jit(solution)/shard_map/while/body/eval_jaxpr/ppermute | solution.py:25
  44.1 7.1 %collective-permute-start = (bf16[1,96,512]{2,1,0:T(8,128)(2,1)S(1)}, bf16[1,96,512]{2,1,0:T(8,128)(2,1)S(1)}, u32[]{:S(2)}, u32[]{:S(2)}) collective-permute-start(bf16[1,96,512]{2,1,0:T(8,128)(2,1)S(1)} %add_bitcast_fusion.8), channel_id=1, source_target_pairs={{0,2},{2,4},{4,6},{6,8},{8,10},{10,12},{12,14},{14,16},{16,18},{18... | collective-permute-start | bytes 294920 | tf_op jit(solution)/shard_map/while/body/eval_jaxpr/ppermute | solution.py:22
  56.3 4.7 %collective-permute-done.3 = bf16[1,96,512]{2,1,0:T(8,128)(2,1)S(1)} collective-permute-done((bf16[1,96,512]{2,1,0:T(8,128)(2,1)S(1)}, bf16[1,96,512]{2,1,0:T(8,128)(2,1)S(1)}, u32[]{:S(2)}, u32[]{:S(2)}) %collective-permute-start.3) | collective-permute-done | bytes 98336 | tf_op jit(solution)/shard_map/while/body/eval_jaxpr/ppermute | solution.py:25
  61.2 2.4 collective-permute-start
  65.1 1.7 collective-permute-start.2
  68.6 5.7 %collective-permute-done.1 = bf16[1,96,512]{2,1,0:T(8,128)(2,1)S(1)} collective-permute-done((bf16[1,96,512]{2,1,0:T(8,128)(2,1)S(1)}, bf16[1,96,512]{2,1,0:T(8,128)(2,1)S(1)}, u32[]{:S(2)}, u32[]{:S(2)}) %collective-permute-start.1) | collective-permute-done | bytes 98336 | tf_op jit(solution)/shard_map/while/body/eval_jaxpr/ppermute | solution.py:25
  74.5 7.8 %collective-permute-start = (bf16[1,96,512]{2,1,0:T(8,128)(2,1)S(1)}, bf16[1,96,512]{2,1,0:T(8,128)(2,1)S(1)}, u32[]{:S(2)}, u32[]{:S(2)}) collective-permute-start(bf16[1,96,512]{2,1,0:T(8,128)(2,1)S(1)} %add_bitcast_fusion.8), channel_id=1, source_target_pairs={{0,2},{2,4},{4,6},{6,8},{8,10},{10,12},{12,14},{14,16},{16,18},{18... | collective-permute-start | bytes 294920 | tf_op jit(solution)/shard_map/while/body/eval_jaxpr/ppermute | solution.py:22
  83.8 1.8 collective-permute-start.2
  88.3 3.8 %collective-permute-done.3 = bf16[1,96,512]{2,1,0:T(8,128)(2,1)S(1)} collective-permute-done((bf16[1,96,512]{2,1,0:T(8,128)(2,1)S(1)}, bf16[1,96,512]{2,1,0:T(8,128)(2,1)S(1)}, u32[]{:S(2)}, u32[]{:S(2)}) %collective-permute-start.3) | collective-permute-done | bytes 98336 | tf_op jit(solution)/shard_map/while/body/eval_jaxpr/ppermute | solution.py:25
  92.4 4.0 %collective-permute-start = (bf16[1,96,512]{2,1,0:T(8,128)(2,1)S(1)}, bf16[1,96,512]{2,1,0:T(8,128)(2,1)S(1)}, u32[]{:S(2)}, u32[]{:S(2)}) collective-permute-start(bf16[1,96,512]{2,1,0:T(8,128)(2,1)S(1)} %add_bitcast_fusion.8), channel_id=1, source_target_pairs={{0,2},{2,4},{4,6},{6,8},{8,10},{10,12},{12,14},{14,16},{16,18},{18... | collective-permute-start | bytes 294920 | tf_op jit(solution)/shard_map/while/body/eval_jaxpr/ppermute | solution.py:22
  97.8 1.8 collective-permute-start.2
  101.3 2.7 collective-permute-done.1
  104.1 2.1 collective-permute-done.3
  106.4 5.7 %collective-permute-start = (bf16[1,96,512]{2,1,0:T(8,128)(2,1)S(1)}, bf16[1,96,512]{2,1,0:T(8,128)(2,1)S(1)}, u32[]{:S(2)}, u32[]{:S(2)}) collective-permute-start(bf16[1,96,512]{2,1,0:T(8,128)(2,1)S(1)} %add_bitcast_fusion.8), channel_id=1, source_target_pairs={{0,2},{2,4},{4,6},{6,8},{8,10},{10,12},{12,14},{14,16},{16,18},{18... | collective-permute-start | bytes 294920 | tf_op jit(solution)/shard_map/while/body/eval_jaxpr/ppermute | solution.py:22
  113.6 1.8 collective-permute-start.2
  118.0 3.9 %collective-permute-done.3 = bf16[1,96,512]{2,1,0:T(8,128)(2,1)S(1)} collective-permute-done((bf16[1,96,512]{2,1,0:T(8,128)(2,1)S(1)}, bf16[1,96,512]{2,1,0:T(8,128)(2,1)S(1)}, u32[]{:S(2)}, u32[]{:S(2)}) %collective-permute-start.3) | collective-permute-done | bytes 98336 | tf_op jit(solution)/shard_map/while/body/eval_jaxpr/ppermute | solution.py:25
  122.1 4.3 %collective-permute-start = (bf16[1,96,512]{2,1,0:T(8,128)(2,1)S(1)}, bf16[1,96,512]{2,1,0:T(8,128)(2,1)S(1)}, u32[]{:S(2)}, u32[]{:S(2)}) collective-permute-start(bf16[1,96,512]{2,1,0:T(8,128)(2,1)S(1)} %add_bitcast_fusion.8), channel_id=1, source_target_pairs={{0,2},{2,4},{4,6},{6,8},{8,10},{10,12},{12,14},{14,16},{16,18},{18... | collective-permute-start | bytes 294920 | tf_op jit(solution)/shard_map/while/body/eval_jaxpr/ppermute | solution.py:22
  127.9 1.8 collective-permute-start.2
  131.5 3.9 %collective-permute-done.1 = bf16[1,96,512]{2,1,0:T(8,128)(2,1)S(1)} collective-permute-done((bf16[1,96,512]{2,1,0:T(8,128)(2,1)S(1)}, bf16[1,96,512]{2,1,0:T(8,128)(2,1)S(1)}, u32[]{:S(2)}, u32[]{:S(2)}) %collective-permute-start.1) | collective-permute-done | bytes 98336 | tf_op jit(solution)/shard_map/while/body/eval_jaxpr/ppermute | solution.py:25
  136.5 6.9 %collective-permute-start = (bf16[1,96,512]{2,1,0:T(8,128)(2,1)S(1)}, bf16[1,96,512]{2,1,0:T(8,128)(2,1)S(1)}, u32[]{:S(2)}, u32[]{:S(2)}) collective-permute-start(bf16[1,96,512]{2,1,0:T(8,128)(2,1)S(1)} %add_bitcast_fusion.8), channel_id=1, source_target_pairs={{0,2},{2,4},{4,6},{6,8},{8,10},{10,12},{12,14},{14,16},{16,18},{18... | collective-permute-start | bytes 294920 | tf_op jit(solution)/shard_map/while/body/eval_jaxpr/ppermute | solution.py:22
  144.8 1.8 collective-permute-start.2
  148.4 1.9 collective-permute-done.1
  150.3 2.9 collective-permute-done.3
  153.4 4.9 %collective-permute-start = (bf16[1,96,512]{2,1,0:T(8,128)(2,1)S(1)}, bf16[1,96,512]{2,1,0:T(8,128)(2,1)S(1)}, u32[]{:S(2)}, u32[]{:S(2)}) collective-permute-start(bf16[1,96,512]{2,1,0:T(8,128)(2,1)S(1)} %add_bitcast_fusion.8), channel_id=1, source_target_pairs={{0,2},{2,4},{4,6},{6,8},{8,10},{10,12},{12,14},{14,16},{16,18},{18... | collective-permute-start | bytes 294920 | tf_op jit(solution)/shard_map/while/body/eval_jaxpr/ppermute | solution.py:22
  159.8 1.8 collective-permute-start.2
  163.3 1.8 collective-permute-done.1
  165.2 2.9 collective-permute-done.3
  168.3 4.9 %collective-permute-start = (bf16[1,96,512]{2,1,0:T(8,128)(2,1)S(1)}, bf16[1,96,512]{2,1,0:T(8,128)(2,1)S(1)}, u32[]{:S(2)}, u32[]{:S(2)}) collective-permute-start(bf16[1,96,512]{2,1,0:T(8,128)(2,1)S(1)} %add_bitcast_fusion.8), channel_id=1, source_target_pairs={{0,2},{2,4},{4,6},{6,8},{8,10},{10,12},{12,14},{14,16},{16,18},{18... | collective-permute-start | bytes 294920 | tf_op jit(solution)/shard_map/while/body/eval_jaxpr/ppermute | solution.py:22
  174.7 1.8 collective-permute-start.2
  178.2 1.8 collective-permute-done.1
  180.1 2.9 collective-permute-done.3
  183.2 4.9 %collective-permute-start = (bf16[1,96,512]{2,1,0:T(8,128)(2,1)S(1)}, bf16[1,96,512]{2,1,0:T(8,128)(2,1)S(1)}, u32[]{:S(2)}, u32[]{:S(2)}) collective-permute-start(bf16[1,96,512]{2,1,0:T(8,128)(2,1)S(1)} %add_bitcast_fusion.8), channel_id=1, source_target_pairs={{0,2},{2,4},{4,6},{6,8},{8,10},{10,12},{12,14},{14,16},{16,18},{18... | collective-permute-start | bytes 294920 | tf_op jit(solution)/shard_map/while/body/eval_jaxpr/ppermute | solution.py:22
  189.6 1.8 collective-permute-start.2
  193.1 1.8 collective-permute-done.1
  195.0 2.9 collective-permute-done.3
  198.1 4.9 %collective-permute-start = (bf16[1,96,512]{2,1,0:T(8,128)(2,1)S(1)}, bf16[1,96,512]{2,1,0:T(8,128)(2,1)S(1)}, u32[]{:S(2)}, u32[]{:S(2)}) collective-permute-start(bf16[1,96,512]{2,1,0:T(8,128)(2,1)S(1)} %add_bitcast_fusion.8), channel_id=1, source_target_pairs={{0,2},{2,4},{4,6},{6,8},{8,10},{10,12},{12,14},{14,16},{16,18},{18... | collective-permute-start | bytes 294920 | tf_op jit(solution)/shard_map/while/body/eval_jaxpr/ppermute | solution.py:22
  204.5 1.8 collective-permute-start.2
  208.0 6.5 %collective-permute-done.1 = bf16[1,96,512]{2,1,0:T(8,128)(2,1)S(1)} collective-permute-done((bf16[1,96,512]{2,1,0:T(8,128)(2,1)S(1)}, bf16[1,96,512]{2,1,0:T(8,128)(2,1)S(1)}, u32[]{:S(2)}, u32[]{:S(2)}) %collective-permute-start.1) | collective-permute-done | bytes 98336 | tf_op jit(solution)/shard_map/while/body/eval_jaxpr/ppermute | solution.py:25
  214.8 17.9 %collective-permute-start = (bf16[1,96,512]{2,1,0:T(8,128)(2,1)S(1)}, bf16[1,96,512]{2,1,0:T(8,128)(2,1)S(1)}, u32[]{:S(2)}, u32[]{:S(2)}) collective-permute-start(bf16[1,96,512]{2,1,0:T(8,128)(2,1)S(1)} %add_bitcast_fusion.8), channel_id=1, source_target_pairs={{0,2},{2,4},{4,6},{6,8},{8,10},{10,12},{12,14},{14,16},{16,18},{18... | collective-permute-start | bytes 294920 | tf_op jit(solution)/shard_map/while/body/eval_jaxpr/ppermute | solution.py:22
  234.2 1.5 collective-permute-start.2
  237.4 7.4 %collective-permute-done.1 = bf16[1,96,512]{2,1,0:T(8,128)(2,1)S(1)} collective-permute-done((bf16[1,96,512]{2,1,0:T(8,128)(2,1)S(1)}, bf16[1,96,512]{2,1,0:T(8,128)(2,1)S(1)}, u32[]{:S(2)}, u32[]{:S(2)}) %collective-permute-start.1) | collective-permute-done | bytes 98336 | tf_op jit(solution)/shard_map/while/body/eval_jaxpr/ppermute | solution.py:25
  245.1 14.6 %collective-permute-start = (bf16[1,96,512]{2,1,0:T(8,128)(2,1)S(1)}, bf16[1,96,512]{2,1,0:T(8,128)(2,1)S(1)}, u32[]{:S(2)}, u32[]{:S(2)}) collective-permute-start(bf16[1,96,512]{2,1,0:T(8,128)(2,1)S(1)} %add_bitcast_fusion.8), channel_id=1, source_target_pairs={{0,2},{2,4},{4,6},{6,8},{8,10},{10,12},{12,14},{14,16},{16,18},{18... | collective-permute-start | bytes 294920 | tf_op jit(solution)/shard_map/while/body/eval_jaxpr/ppermute | solution.py:22
  261.2 1.7 collective-permute-start.2
  264.5 8.9 %collective-permute-done.1 = bf16[1,96,512]{2,1,0:T(8,128)(2,1)S(1)} collective-permute-done((bf16[1,96,512]{2,1,0:T(8,128)(2,1)S(1)}, bf16[1,96,512]{2,1,0:T(8,128)(2,1)S(1)}, u32[]{:S(2)}, u32[]{:S(2)}) %collective-permute-start.1) | collective-permute-done | bytes 98336 | tf_op jit(solution)/shard_map/while/body/eval_jaxpr/ppermute | solution.py:25
  273.7 8.0 %collective-permute-start = (bf16[1,96,512]{2,1,0:T(8,128)(2,1)S(1)}, bf16[1,96,512]{2,1,0:T(8,128)(2,1)S(1)}, u32[]{:S(2)}, u32[]{:S(2)}) collective-permute-start(bf16[1,96,512]{2,1,0:T(8,128)(2,1)S(1)} %add_bitcast_fusion.8), channel_id=1, source_target_pairs={{0,2},{2,4},{4,6},{6,8},{8,10},{10,12},{12,14},{14,16},{16,18},{18... | collective-permute-start | bytes 294920 | tf_op jit(solution)/shard_map/while/body/eval_jaxpr/ppermute | solution.py:22
  281.7 5.1 %conditional.14 = (bf16[96,512]{1,0:T(8,128)(2,1)S(1)}, bf16[96,512]{1,0:T(8,128)(2,1)S(1)}) conditional(s32[]{:T(128)} %convert_element_type.92, () %tuple.104, (f32[96,2048]{1,0:T(8,128)S(1)}, bf16[2048,2048]{1,0:T(8,128)(2,1)}, bf16[96,512]{1,0:T(8,128)(2,1)S(1)}, bf16[96,512]{1,0:T(8,128)(2,1)S(1)}) %tuple.105), branch_computations={%region_5.5_spmd, %region_6.6_spmd} | conditional | flops 201621504 | bytes 3866640 | solution.py:103
  288.2 1.8 collective-permute-start.2
  291.7 4.2 %collective-permute-done.1 = bf16[1,96,512]{2,1,0:T(8,128)(2,1)S(1)} collective-permute-done((bf16[1,96,512]{2,1,0:T(8,128)(2,1)S(1)}, bf16[1,96,512]{2,1,0:T(8,128)(2,1)S(1)}, u32[]{:S(2)}, u32[]{:S(2)}) %collective-permute-start.1) | collective-permute-done | bytes 98336 | tf_op jit(solution)/shard_map/while/body/eval_jaxpr/ppermute | solution.py:25
  296.8 7.2 %collective-permute-start = (bf16[1,96,512]{2,1,0:T(8,128)(2,1)S(1)}, bf16[1,96,512]{2,1,0:T(8,128)(2,1)S(1)}, u32[]{:S(2)}, u32[]{:S(2)}) collective-permute-start(bf16[1,96,512]{2,1,0:T(8,128)(2,1)S(1)} %add_bitcast_fusion.8), channel_id=1, source_target_pairs={{0,2},{2,4},{4,6},{6,8},{8,10},{10,12},{12,14},{14,16},{16,18},{18... | collective-permute-start | bytes 294920 | tf_op jit(solution)/shard_map/while/body/eval_jaxpr/ppermute | solution.py:22
  304.0 5.1 %conditional.15 = (bf16[96,512]{1,0:T(8,128)(2,1)S(1)}, bf16[96,512]{1,0:T(8,128)(2,1)S(1)}) conditional(s32[]{:T(128)} %convert_element_type.93, () %tuple.106, (f32[96,2048]{1,0:T(8,128)S(1)}, bf16[2048,2048]{1,0:T(8,128)(2,1)}, bf16[96,512]{1,0:T(8,128)(2,1)S(1)}, bf16[96,512]{1,0:T(8,128)(2,1)S(1)}) %tuple.107), branch_computations={%region_7.7_spmd, %region_8.8_spmd} | conditional | flops 201621504 | bytes 3866640 | solution.py:103
  310.5 1.8 collective-permute-start.2
  315.3 4.4 %collective-permute-done.3 = bf16[1,96,512]{2,1,0:T(8,128)(2,1)S(1)} collective-permute-done((bf16[1,96,512]{2,1,0:T(8,128)(2,1)S(1)}, bf16[1,96,512]{2,1,0:T(8,128)(2,1)S(1)}, u32[]{:S(2)}, u32[]{:S(2)}) %collective-permute-start.3) | collective-permute-done | bytes 98336 | tf_op jit(solution)/shard_map/while/body/eval_jaxpr/ppermute | solution.py:25
  319.8 2.2 convolution_add_fusion.23
  322.0 2.5 convolution_add_fusion.22
  324.5 2.1 convolution_add_fusion.21
  329.1 1.9 collective-permute-start.4
  336.6 4.7 %collective-permute-done.7 = bf16[1,1,96,512]{3,2,1,0:T(8,128)(2,1)S(1)} collective-permute-done((bf16[1,1,96,512]{3,2,1,0:T(8,128)(2,1)S(1)}, bf16[1,1,96,512]{3,2,1,0:T(8,128)(2,1)S(1)}, u32[]{:S(2)}, u32[]{:S(2)}) %collective-permute-start.7) | collective-permute-done | bytes 98336 | tf_op jit(solution)/shard_map/ppermute | solution.py:25
  (603 shorter events, 96.7 us)
Async XLA Ops:
  11.1 9.4 %collective-permute-start = (bf16[1,96,512]{2,1,0:T(8,128)(2,1)S(1)}, bf16[1,96,512]{2,1,0:T(8,128)(2,1)S(1)}, u32[]{:S(2)}, u32[]{:S(2)}) collective-permute-start(bf16[1,96,512]{2,1,0:T(8,128)(2,1)S(1)} %add_bitcast_fusion.8), channel_id=1, source_target_pairs={{0,2},{2,4},{4,6},{6,8},{8,10},{10,12},{12,14},{14,16},{16,18},{18... | collective-permute-start | bytes 294920 | tf_op jit(solution)/shard_map/while/body/eval_jaxpr/ppermute | solution.py:22
  12.6 7.9 %collective-permute-start.1 = (bf16[1,96,512]{2,1,0:T(8,128)(2,1)S(1)}, bf16[1,96,512]{2,1,0:T(8,128)(2,1)S(1)}, u32[]{:S(2)}, u32[]{:S(2)}) collective-permute-start(bf16[1,96,512]{2,1,0:T(8,128)(2,1)S(1)} %add_bitcast_fusion.9), channel_id=1, source_target_pairs={{2,0},{4,2},{6,4},{8,6},{10,8},{12,10},{14,12},{16,14},{18,16},{20... | collective-permute-start | bytes 294920 | tf_op jit(solution)/shard_map/while/body/eval_jaxpr/ppermute | solution.py:25
  13.9 7.9 %collective-permute-start.2 = (bf16[1,96,512]{2,1,0:T(8,128)(2,1)S(1)}, bf16[1,96,512]{2,1,0:T(8,128)(2,1)S(1)}, u32[]{:S(2)}, u32[]{:S(2)}) collective-permute-start(bf16[1,96,512]{2,1,0:T(8,128)(2,1)S(1)} %add_bitcast_fusion.10), channel_id=1, source_target_pairs={{0,1},{2,3},{4,5},{6,7},{8,9},{10,11},{12,13},{14,15},{16,17},{18,... | collective-permute-start | bytes 294920 | tf_op jit(solution)/shard_map/while/body/eval_jaxpr/ppermute | solution.py:22
  18.8 7.4 %collective-permute-start.3 = (bf16[1,96,512]{2,1,0:T(8,128)(2,1)S(1)}, bf16[1,96,512]{2,1,0:T(8,128)(2,1)S(1)}, u32[]{:S(2)}, u32[]{:S(2)}) collective-permute-start(bf16[1,96,512]{2,1,0:T(8,128)(2,1)S(1)} %add_bitcast_fusion.11), channel_id=1, source_target_pairs={{1,0},{3,2},{5,4},{7,6},{9,8},{11,10},{13,12},{15,14},{17,16},{19,... | collective-permute-start | bytes 294920 | tf_op jit(solution)/shard_map/while/body/eval_jaxpr/ppermute | solution.py:25
  31.5 6.5 %collective-permute-start = (bf16[1,96,512]{2,1,0:T(8,128)(2,1)S(1)}, bf16[1,96,512]{2,1,0:T(8,128)(2,1)S(1)}, u32[]{:S(2)}, u32[]{:S(2)}) collective-permute-start(bf16[1,96,512]{2,1,0:T(8,128)(2,1)S(1)} %add_bitcast_fusion.8), channel_id=1, source_target_pairs={{0,2},{2,4},{4,6},{6,8},{8,10},{10,12},{12,14},{14,16},{16,18},{18... | collective-permute-start | bytes 294920 | tf_op jit(solution)/shard_map/while/body/eval_jaxpr/ppermute | solution.py:22
  36.4 7.6 %collective-permute-start.3 = (bf16[1,96,512]{2,1,0:T(8,128)(2,1)S(1)}, bf16[1,96,512]{2,1,0:T(8,128)(2,1)S(1)}, u32[]{:S(2)}, u32[]{:S(2)}) collective-permute-start(bf16[1,96,512]{2,1,0:T(8,128)(2,1)S(1)} %add_bitcast_fusion.11), channel_id=1, source_target_pairs={{1,0},{3,2},{5,4},{7,6},{9,8},{11,10},{13,12},{15,14},{17,16},{19,... | collective-permute-start | bytes 294920 | tf_op jit(solution)/shard_map/while/body/eval_jaxpr/ppermute | solution.py:25
  44.1 11.7 %collective-permute-start = (bf16[1,96,512]{2,1,0:T(8,128)(2,1)S(1)}, bf16[1,96,512]{2,1,0:T(8,128)(2,1)S(1)}, u32[]{:S(2)}, u32[]{:S(2)}) collective-permute-start(bf16[1,96,512]{2,1,0:T(8,128)(2,1)S(1)} %add_bitcast_fusion.8), channel_id=1, source_target_pairs={{0,2},{2,4},{4,6},{6,8},{8,10},{10,12},{12,14},{14,16},{16,18},{18... | collective-permute-start | bytes 294920 | tf_op jit(solution)/shard_map/while/body/eval_jaxpr/ppermute | solution.py:22
  54.1 6.9 %collective-permute-start.3 = (bf16[1,96,512]{2,1,0:T(8,128)(2,1)S(1)}, bf16[1,96,512]{2,1,0:T(8,128)(2,1)S(1)}, u32[]{:S(2)}, u32[]{:S(2)}) collective-permute-start(bf16[1,96,512]{2,1,0:T(8,128)(2,1)S(1)} %add_bitcast_fusion.11), channel_id=1, source_target_pairs={{1,0},{3,2},{5,4},{7,6},{9,8},{11,10},{13,12},{15,14},{17,16},{19,... | collective-permute-start | bytes 294920 | tf_op jit(solution)/shard_map/while/body/eval_jaxpr/ppermute | solution.py:25
  61.2 7.3 %collective-permute-start = (bf16[1,96,512]{2,1,0:T(8,128)(2,1)S(1)}, bf16[1,96,512]{2,1,0:T(8,128)(2,1)S(1)}, u32[]{:S(2)}, u32[]{:S(2)}) collective-permute-start(bf16[1,96,512]{2,1,0:T(8,128)(2,1)S(1)} %add_bitcast_fusion.8), channel_id=1, source_target_pairs={{0,2},{2,4},{4,6},{6,8},{8,10},{10,12},{12,14},{14,16},{16,18},{18... | collective-permute-start | bytes 294920 | tf_op jit(solution)/shard_map/while/body/eval_jaxpr/ppermute | solution.py:22
  63.8 10.5 %collective-permute-start.1 = (bf16[1,96,512]{2,1,0:T(8,128)(2,1)S(1)}, bf16[1,96,512]{2,1,0:T(8,128)(2,1)S(1)}, u32[]{:S(2)}, u32[]{:S(2)}) collective-permute-start(bf16[1,96,512]{2,1,0:T(8,128)(2,1)S(1)} %add_bitcast_fusion.9), channel_id=1, source_target_pairs={{2,0},{4,2},{6,4},{8,6},{10,8},{12,10},{14,12},{16,14},{18,16},{20... | collective-permute-start | bytes 294920 | tf_op jit(solution)/shard_map/while/body/eval_jaxpr/ppermute | solution.py:25
  65.1 9.2 %collective-permute-start.2 = (bf16[1,96,512]{2,1,0:T(8,128)(2,1)S(1)}, bf16[1,96,512]{2,1,0:T(8,128)(2,1)S(1)}, u32[]{:S(2)}, u32[]{:S(2)}) collective-permute-start(bf16[1,96,512]{2,1,0:T(8,128)(2,1)S(1)} %add_bitcast_fusion.10), channel_id=1, source_target_pairs={{0,1},{2,3},{4,5},{6,7},{8,9},{10,11},{12,13},{14,15},{16,17},{18,... | collective-permute-start | bytes 294920 | tf_op jit(solution)/shard_map/while/body/eval_jaxpr/ppermute | solution.py:22
  66.9 7.5 %collective-permute-start.3 = (bf16[1,96,512]{2,1,0:T(8,128)(2,1)S(1)}, bf16[1,96,512]{2,1,0:T(8,128)(2,1)S(1)}, u32[]{:S(2)}, u32[]{:S(2)}) collective-permute-start(bf16[1,96,512]{2,1,0:T(8,128)(2,1)S(1)} %add_bitcast_fusion.11), channel_id=1, source_target_pairs={{1,0},{3,2},{5,4},{7,6},{9,8},{11,10},{13,12},{15,14},{17,16},{19,... | collective-permute-start | bytes 294920 | tf_op jit(solution)/shard_map/while/body/eval_jaxpr/ppermute | solution.py:25
  74.5 12.7 %collective-permute-start = (bf16[1,96,512]{2,1,0:T(8,128)(2,1)S(1)}, bf16[1,96,512]{2,1,0:T(8,128)(2,1)S(1)}, u32[]{:S(2)}, u32[]{:S(2)}) collective-permute-start(bf16[1,96,512]{2,1,0:T(8,128)(2,1)S(1)} %add_bitcast_fusion.8), channel_id=1, source_target_pairs={{0,2},{2,4},{4,6},{6,8},{8,10},{10,12},{12,14},{14,16},{16,18},{18... | collective-permute-start | bytes 294920 | tf_op jit(solution)/shard_map/while/body/eval_jaxpr/ppermute | solution.py:22
  82.5 5.8 %collective-permute-start.1 = (bf16[1,96,512]{2,1,0:T(8,128)(2,1)S(1)}, bf16[1,96,512]{2,1,0:T(8,128)(2,1)S(1)}, u32[]{:S(2)}, u32[]{:S(2)}) collective-permute-start(bf16[1,96,512]{2,1,0:T(8,128)(2,1)S(1)} %add_bitcast_fusion.9), channel_id=1, source_target_pairs={{2,0},{4,2},{6,4},{8,6},{10,8},{12,10},{14,12},{16,14},{18,16},{20... | collective-permute-start | bytes 294920 | tf_op jit(solution)/shard_map/while/body/eval_jaxpr/ppermute | solution.py:25
  85.6 6.5 %collective-permute-start.3 = (bf16[1,96,512]{2,1,0:T(8,128)(2,1)S(1)}, bf16[1,96,512]{2,1,0:T(8,128)(2,1)S(1)}, u32[]{:S(2)}, u32[]{:S(2)}) collective-permute-start(bf16[1,96,512]{2,1,0:T(8,128)(2,1)S(1)} %add_bitcast_fusion.11), channel_id=1, source_target_pairs={{1,0},{3,2},{5,4},{7,6},{9,8},{11,10},{13,12},{15,14},{17,16},{19,... | collective-permute-start | bytes 294920 | tf_op jit(solution)/shard_map/while/body/eval_jaxpr/ppermute | solution.py:25
  92.4 8.9 %collective-permute-start = (bf16[1,96,512]{2,1,0:T(8,128)(2,1)S(1)}, bf16[1,96,512]{2,1,0:T(8,128)(2,1)S(1)}, u32[]{:S(2)}, u32[]{:S(2)}) collective-permute-start(bf16[1,96,512]{2,1,0:T(8,128)(2,1)S(1)} %add_bitcast_fusion.8), channel_id=1, source_target_pairs={{0,2},{2,4},{4,6},{6,8},{8,10},{10,12},{12,14},{14,16},{16,18},{18... | collective-permute-start | bytes 294920 | tf_op jit(solution)/shard_map/while/body/eval_jaxpr/ppermute | solution.py:22
  96.5 7.6 %collective-permute-start.1 = (bf16[1,96,512]{2,1,0:T(8,128)(2,1)S(1)}, bf16[1,96,512]{2,1,0:T(8,128)(2,1)S(1)}, u32[]{:S(2)}, u32[]{:S(2)}) collective-permute-start(bf16[1,96,512]{2,1,0:T(8,128)(2,1)S(1)} %add_bitcast_fusion.9), channel_id=1, source_target_pairs={{2,0},{4,2},{6,4},{8,6},{10,8},{12,10},{14,12},{16,14},{18,16},{20... | collective-permute-start | bytes 294920 | tf_op jit(solution)/shard_map/while/body/eval_jaxpr/ppermute | solution.py:25
  97.8 6.3 %collective-permute-start.2 = (bf16[1,96,512]{2,1,0:T(8,128)(2,1)S(1)}, bf16[1,96,512]{2,1,0:T(8,128)(2,1)S(1)}, u32[]{:S(2)}, u32[]{:S(2)}) collective-permute-start(bf16[1,96,512]{2,1,0:T(8,128)(2,1)S(1)} %add_bitcast_fusion.10), channel_id=1, source_target_pairs={{0,1},{2,3},{4,5},{6,7},{8,9},{10,11},{12,13},{14,15},{16,17},{18,... | collective-permute-start | bytes 294920 | tf_op jit(solution)/shard_map/while/body/eval_jaxpr/ppermute | solution.py:22
  99.7 6.5 %collective-permute-start.3 = (bf16[1,96,512]{2,1,0:T(8,128)(2,1)S(1)}, bf16[1,96,512]{2,1,0:T(8,128)(2,1)S(1)}, u32[]{:S(2)}, u32[]{:S(2)}) collective-permute-start(bf16[1,96,512]{2,1,0:T(8,128)(2,1)S(1)} %add_bitcast_fusion.11), channel_id=1, source_target_pairs={{1,0},{3,2},{5,4},{7,6},{9,8},{11,10},{13,12},{15,14},{17,16},{19,... | collective-permute-start | bytes 294920 | tf_op jit(solution)/shard_map/while/body/eval_jaxpr/ppermute | solution.py:25
  106.4 10.7 %collective-permute-start = (bf16[1,96,512]{2,1,0:T(8,128)(2,1)S(1)}, bf16[1,96,512]{2,1,0:T(8,128)(2,1)S(1)}, u32[]{:S(2)}, u32[]{:S(2)}) collective-permute-start(bf16[1,96,512]{2,1,0:T(8,128)(2,1)S(1)} %add_bitcast_fusion.8), channel_id=1, source_target_pairs={{0,2},{2,4},{4,6},{6,8},{8,10},{10,12},{12,14},{14,16},{16,18},{18... | collective-permute-start | bytes 294920 | tf_op jit(solution)/shard_map/while/body/eval_jaxpr/ppermute | solution.py:22
  112.2 5.7 %collective-permute-start.1 = (bf16[1,96,512]{2,1,0:T(8,128)(2,1)S(1)}, bf16[1,96,512]{2,1,0:T(8,128)(2,1)S(1)}, u32[]{:S(2)}, u32[]{:S(2)}) collective-permute-start(bf16[1,96,512]{2,1,0:T(8,128)(2,1)S(1)} %add_bitcast_fusion.9), channel_id=1, source_target_pairs={{2,0},{4,2},{6,4},{8,6},{10,8},{12,10},{14,12},{16,14},{18,16},{20... | collective-permute-start | bytes 294920 | tf_op jit(solution)/shard_map/while/body/eval_jaxpr/ppermute | solution.py:25
  115.4 6.5 %collective-permute-start.3 = (bf16[1,96,512]{2,1,0:T(8,128)(2,1)S(1)}, bf16[1,96,512]{2,1,0:T(8,128)(2,1)S(1)}, u32[]{:S(2)}, u32[]{:S(2)}) collective-permute-start(bf16[1,96,512]{2,1,0:T(8,128)(2,1)S(1)} %add_bitcast_fusion.11), channel_id=1, source_target_pairs={{1,0},{3,2},{5,4},{7,6},{9,8},{11,10},{13,12},{15,14},{17,16},{19,... | collective-permute-start | bytes 294920 | tf_op jit(solution)/shard_map/while/body/eval_jaxpr/ppermute | solution.py:25
  122.1 9.3 %collective-permute-start = (bf16[1,96,512]{2,1,0:T(8,128)(2,1)S(1)}, bf16[1,96,512]{2,1,0:T(8,128)(2,1)S(1)}, u32[]{:S(2)}, u32[]{:S(2)}) collective-permute-start(bf16[1,96,512]{2,1,0:T(8,128)(2,1)S(1)} %add_bitcast_fusion.8), channel_id=1, source_target_pairs={{0,2},{2,4},{4,6},{6,8},{8,10},{10,12},{12,14},{14,16},{16,18},{18... | collective-permute-start | bytes 294920 | tf_op jit(solution)/shard_map/while/body/eval_jaxpr/ppermute | solution.py:22
  126.6 8.7 %collective-permute-start.1 = (bf16[1,96,512]{2,1,0:T(8,128)(2,1)S(1)}, bf16[1,96,512]{2,1,0:T(8,128)(2,1)S(1)}, u32[]{:S(2)}, u32[]{:S(2)}) collective-permute-start(bf16[1,96,512]{2,1,0:T(8,128)(2,1)S(1)} %add_bitcast_fusion.9), channel_id=1, source_target_pairs={{2,0},{4,2},{6,4},{8,6},{10,8},{12,10},{14,12},{16,14},{18,16},{20... | collective-permute-start | bytes 294920 | tf_op jit(solution)/shard_map/while/body/eval_jaxpr/ppermute | solution.py:25
  127.9 7.4 %collective-permute-start.2 = (bf16[1,96,512]{2,1,0:T(8,128)(2,1)S(1)}, bf16[1,96,512]{2,1,0:T(8,128)(2,1)S(1)}, u32[]{:S(2)}, u32[]{:S(2)}) collective-permute-start(bf16[1,96,512]{2,1,0:T(8,128)(2,1)S(1)} %add_bitcast_fusion.10), channel_id=1, source_target_pairs={{0,1},{2,3},{4,5},{6,7},{8,9},{10,11},{12,13},{14,15},{16,17},{18,... | collective-permute-start | bytes 294920 | tf_op jit(solution)/shard_map/while/body/eval_jaxpr/ppermute | solution.py:22
  129.8 6.5 %collective-permute-start.3 = (bf16[1,96,512]{2,1,0:T(8,128)(2,1)S(1)}, bf16[1,96,512]{2,1,0:T(8,128)(2,1)S(1)}, u32[]{:S(2)}, u32[]{:S(2)}) collective-permute-start(bf16[1,96,512]{2,1,0:T(8,128)(2,1)S(1)} %add_bitcast_fusion.11), channel_id=1, source_target_pairs={{1,0},{3,2},{5,4},{7,6},{9,8},{11,10},{13,12},{15,14},{17,16},{19,... | collective-permute-start | bytes 294920 | tf_op jit(solution)/shard_map/while/body/eval_jaxpr/ppermute | solution.py:25
  136.5 11.9 %collective-permute-start = (bf16[1,96,512]{2,1,0:T(8,128)(2,1)S(1)}, bf16[1,96,512]{2,1,0:T(8,128)(2,1)S(1)}, u32[]{:S(2)}, u32[]{:S(2)}) collective-permute-start(bf16[1,96,512]{2,1,0:T(8,128)(2,1)S(1)} %add_bitcast_fusion.8), channel_id=1, source_target_pairs={{0,2},{2,4},{4,6},{6,8},{8,10},{10,12},{12,14},{14,16},{16,18},{18... | collective-permute-start | bytes 294920 | tf_op jit(solution)/shard_map/while/body/eval_jaxpr/ppermute | solution.py:22
  143.5 6.7 %collective-permute-start.1 = (bf16[1,96,512]{2,1,0:T(8,128)(2,1)S(1)}, bf16[1,96,512]{2,1,0:T(8,128)(2,1)S(1)}, u32[]{:S(2)}, u32[]{:S(2)}) collective-permute-start(bf16[1,96,512]{2,1,0:T(8,128)(2,1)S(1)} %add_bitcast_fusion.9), channel_id=1, source_target_pairs={{2,0},{4,2},{6,4},{8,6},{10,8},{12,10},{14,12},{16,14},{18,16},{20... | collective-permute-start | bytes 294920 | tf_op jit(solution)/shard_map/while/body/eval_jaxpr/ppermute | solution.py:25
  144.8 5.4 %collective-permute-start.2 = (bf16[1,96,512]{2,1,0:T(8,128)(2,1)S(1)}, bf16[1,96,512]{2,1,0:T(8,128)(2,1)S(1)}, u32[]{:S(2)}, u32[]{:S(2)}) collective-permute-start(bf16[1,96,512]{2,1,0:T(8,128)(2,1)S(1)} %add_bitcast_fusion.10), channel_id=1, source_target_pairs={{0,1},{2,3},{4,5},{6,7},{8,9},{10,11},{12,13},{14,15},{16,17},{18,... | collective-permute-start | bytes 294920 | tf_op jit(solution)/shard_map/while/body/eval_jaxpr/ppermute | solution.py:22
  146.7 6.5 %collective-permute-start.3 = (bf16[1,96,512]{2,1,0:T(8,128)(2,1)S(1)}, bf16[1,96,512]{2,1,0:T(8,128)(2,1)S(1)}, u32[]{:S(2)}, u32[]{:S(2)}) collective-permute-start(bf16[1,96,512]{2,1,0:T(8,128)(2,1)S(1)} %add_bitcast_fusion.11), channel_id=1, source_target_pairs={{1,0},{3,2},{5,4},{7,6},{9,8},{11,10},{13,12},{15,14},{17,16},{19,... | collective-permute-start | bytes 294920 | tf_op jit(solution)/shard_map/while/body/eval_jaxpr/ppermute | solution.py:25
  153.4 9.8 %collective-permute-start = (bf16[1,96,512]{2,1,0:T(8,128)(2,1)S(1)}, bf16[1,96,512]{2,1,0:T(8,128)(2,1)S(1)}, u32[]{:S(2)}, u32[]{:S(2)}) collective-permute-start(bf16[1,96,512]{2,1,0:T(8,128)(2,1)S(1)} %add_bitcast_fusion.8), channel_id=1, source_target_pairs={{0,2},{2,4},{4,6},{6,8},{8,10},{10,12},{12,14},{14,16},{16,18},{18... | collective-permute-start | bytes 294920 | tf_op jit(solution)/shard_map/while/body/eval_jaxpr/ppermute | solution.py:22
  158.4 6.7 %collective-permute-start.1 = (bf16[1,96,512]{2,1,0:T(8,128)(2,1)S(1)}, bf16[1,96,512]{2,1,0:T(8,128)(2,1)S(1)}, u32[]{:S(2)}, u32[]{:S(2)}) collective-permute-start(bf16[1,96,512]{2,1,0:T(8,128)(2,1)S(1)} %add_bitcast_fusion.9), channel_id=1, source_target_pairs={{2,0},{4,2},{6,4},{8,6},{10,8},{12,10},{14,12},{16,14},{18,16},{20... | collective-permute-start | bytes 294920 | tf_op jit(solution)/shard_map/while/body/eval_jaxpr/ppermute | solution.py:25
  159.8 5.4 %collective-permute-start.2 = (bf16[1,96,512]{2,1,0:T(8,128)(2,1)S(1)}, bf16[1,96,512]{2,1,0:T(8,128)(2,1)S(1)}, u32[]{:S(2)}, u32[]{:S(2)}) collective-permute-start(bf16[1,96,512]{2,1,0:T(8,128)(2,1)S(1)} %add_bitcast_fusion.10), channel_id=1, source_target_pairs={{0,1},{2,3},{4,5},{6,7},{8,9},{10,11},{12,13},{14,15},{16,17},{18,... | collective-permute-start | bytes 294920 | tf_op jit(solution)/shard_map/while/body/eval_jaxpr/ppermute | solution.py:22
  161.6 6.5 %collective-permute-start.3 = (bf16[1,96,512]{2,1,0:T(8,128)(2,1)S(1)}, bf16[1,96,512]{2,1,0:T(8,128)(2,1)S(1)}, u32[]{:S(2)}, u32[]{:S(2)}) collective-permute-start(bf16[1,96,512]{2,1,0:T(8,128)(2,1)S(1)} %add_bitcast_fusion.11), channel_id=1, source_target_pairs={{1,0},{3,2},{5,4},{7,6},{9,8},{11,10},{13,12},{15,14},{17,16},{19,... | collective-permute-start | bytes 294920 | tf_op jit(solution)/shard_map/while/body/eval_jaxpr/ppermute | solution.py:25
  168.3 9.8 %collective-permute-start = (bf16[1,96,512]{2,1,0:T(8,128)(2,1)S(1)}, bf16[1,96,512]{2,1,0:T(8,128)(2,1)S(1)}, u32[]{:S(2)}, u32[]{:S(2)}) collective-permute-start(bf16[1,96,512]{2,1,0:T(8,128)(2,1)S(1)} %add_bitcast_fusion.8), channel_id=1, source_target_pairs={{0,2},{2,4},{4,6},{6,8},{8,10},{10,12},{12,14},{14,16},{16,18},{18... | collective-permute-start | bytes 294920 | tf_op jit(solution)/shard_map/while/body/eval_jaxpr/ppermute | solution.py:22
  173.4 6.7 %collective-permute-start.1 = (bf16[1,96,512]{2,1,0:T(8,128)(2,1)S(1)}, bf16[1,96,512]{2,1,0:T(8,128)(2,1)S(1)}, u32[]{:S(2)}, u32[]{:S(2)}) collective-permute-start(bf16[1,96,512]{2,1,0:T(8,128)(2,1)S(1)} %add_bitcast_fusion.9), channel_id=1, source_target_pairs={{2,0},{4,2},{6,4},{8,6},{10,8},{12,10},{14,12},{16,14},{18,16},{20... | collective-permute-start | bytes 294920 | tf_op jit(solution)/shard_map/while/body/eval_jaxpr/ppermute | solution.py:25
  174.7 5.4 %collective-permute-start.2 = (bf16[1,96,512]{2,1,0:T(8,128)(2,1)S(1)}, bf16[1,96,512]{2,1,0:T(8,128)(2,1)S(1)}, u32[]{:S(2)}, u32[]{:S(2)}) collective-permute-start(bf16[1,96,512]{2,1,0:T(8,128)(2,1)S(1)} %add_bitcast_fusion.10), channel_id=1, source_target_pairs={{0,1},{2,3},{4,5},{6,7},{8,9},{10,11},{12,13},{14,15},{16,17},{18,... | collective-permute-start | bytes 294920 | tf_op jit(solution)/shard_map/while/body/eval_jaxpr/ppermute | solution.py:22
  176.5 6.5 %collective-permute-start.3 = (bf16[1,96,512]{2,1,0:T(8,128)(2,1)S(1)}, bf16[1,96,512]{2,1,0:T(8,128)(2,1)S(1)}, u32[]{:S(2)}, u32[]{:S(2)}) collective-permute-start(bf16[1,96,512]{2,1,0:T(8,128)(2,1)S(1)} %add_bitcast_fusion.11), channel_id=1, source_target_pairs={{1,0},{3,2},{5,4},{7,6},{9,8},{11,10},{13,12},{15,14},{17,16},{19,... | collective-permute-start | bytes 294920 | tf_op jit(solution)/shard_map/while/body/eval_jaxpr/ppermute | solution.py:25
  183.2 9.8 %collective-permute-start = (bf16[1,96,512]{2,1,0:T(8,128)(2,1)S(1)}, bf16[1,96,512]{2,1,0:T(8,128)(2,1)S(1)}, u32[]{:S(2)}, u32[]{:S(2)}) collective-permute-start(bf16[1,96,512]{2,1,0:T(8,128)(2,1)S(1)} %add_bitcast_fusion.8), channel_id=1, source_target_pairs={{0,2},{2,4},{4,6},{6,8},{8,10},{10,12},{12,14},{14,16},{16,18},{18... | collective-permute-start | bytes 294920 | tf_op jit(solution)/shard_map/while/body/eval_jaxpr/ppermute | solution.py:22
  188.3 6.7 %collective-permute-start.1 = (bf16[1,96,512]{2,1,0:T(8,128)(2,1)S(1)}, bf16[1,96,512]{2,1,0:T(8,128)(2,1)S(1)}, u32[]{:S(2)}, u32[]{:S(2)}) collective-permute-start(bf16[1,96,512]{2,1,0:T(8,128)(2,1)S(1)} %add_bitcast_fusion.9), channel_id=1, source_target_pairs={{2,0},{4,2},{6,4},{8,6},{10,8},{12,10},{14,12},{16,14},{18,16},{20... | collective-permute-start | bytes 294920 | tf_op jit(solution)/shard_map/while/body/eval_jaxpr/ppermute | solution.py:25
  189.6 5.4 %collective-permute-start.2 = (bf16[1,96,512]{2,1,0:T(8,128)(2,1)S(1)}, bf16[1,96,512]{2,1,0:T(8,128)(2,1)S(1)}, u32[]{:S(2)}, u32[]{:S(2)}) collective-permute-start(bf16[1,96,512]{2,1,0:T(8,128)(2,1)S(1)} %add_bitcast_fusion.10), channel_id=1, source_target_pairs={{0,1},{2,3},{4,5},{6,7},{8,9},{10,11},{12,13},{14,15},{16,17},{18,... | collective-permute-start | bytes 294920 | tf_op jit(solution)/shard_map/while/body/eval_jaxpr/ppermute | solution.py:22
  191.4 6.5 %collective-permute-start.3 = (bf16[1,96,512]{2,1,0:T(8,128)(2,1)S(1)}, bf16[1,96,512]{2,1,0:T(8,128)(2,1)S(1)}, u32[]{:S(2)}, u32[]{:S(2)}) collective-permute-start(bf16[1,96,512]{2,1,0:T(8,128)(2,1)S(1)} %add_bitcast_fusion.11), channel_id=1, source_target_pairs={{1,0},{3,2},{5,4},{7,6},{9,8},{11,10},{13,12},{15,14},{17,16},{19,... | collective-permute-start | bytes 294920 | tf_op jit(solution)/shard_map/while/body/eval_jaxpr/ppermute | solution.py:25
  198.1 9.8 %collective-permute-start = (bf16[1,96,512]{2,1,0:T(8,128)(2,1)S(1)}, bf16[1,96,512]{2,1,0:T(8,128)(2,1)S(1)}, u32[]{:S(2)}, u32[]{:S(2)}) collective-permute-start(bf16[1,96,512]{2,1,0:T(8,128)(2,1)S(1)} %add_bitcast_fusion.8), channel_id=1, source_target_pairs={{0,2},{2,4},{4,6},{6,8},{8,10},{10,12},{12,14},{14,16},{16,18},{18... | collective-permute-start | bytes 294920 | tf_op jit(solution)/shard_map/while/body/eval_jaxpr/ppermute | solution.py:22
  203.2 11.3 %collective-permute-start.1 = (bf16[1,96,512]{2,1,0:T(8,128)(2,1)S(1)}, bf16[1,96,512]{2,1,0:T(8,128)(2,1)S(1)}, u32[]{:S(2)}, u32[]{:S(2)}) collective-permute-start(bf16[1,96,512]{2,1,0:T(8,128)(2,1)S(1)} %add_bitcast_fusion.9), channel_id=1, source_target_pairs={{2,0},{4,2},{6,4},{8,6},{10,8},{12,10},{14,12},{16,14},{18,16},{20... | collective-permute-start | bytes 294920 | tf_op jit(solution)/shard_map/while/body/eval_jaxpr/ppermute | solution.py:25
  204.5 10.0 %collective-permute-start.2 = (bf16[1,96,512]{2,1,0:T(8,128)(2,1)S(1)}, bf16[1,96,512]{2,1,0:T(8,128)(2,1)S(1)}, u32[]{:S(2)}, u32[]{:S(2)}) collective-permute-start(bf16[1,96,512]{2,1,0:T(8,128)(2,1)S(1)} %add_bitcast_fusion.10), channel_id=1, source_target_pairs={{0,1},{2,3},{4,5},{6,7},{8,9},{10,11},{12,13},{14,15},{16,17},{18,... | collective-permute-start | bytes 294920 | tf_op jit(solution)/shard_map/while/body/eval_jaxpr/ppermute | solution.py:22
  206.3 8.2 %collective-permute-start.3 = (bf16[1,96,512]{2,1,0:T(8,128)(2,1)S(1)}, bf16[1,96,512]{2,1,0:T(8,128)(2,1)S(1)}, u32[]{:S(2)}, u32[]{:S(2)}) collective-permute-start(bf16[1,96,512]{2,1,0:T(8,128)(2,1)S(1)} %add_bitcast_fusion.11), channel_id=1, source_target_pairs={{1,0},{3,2},{5,4},{7,6},{9,8},{11,10},{13,12},{15,14},{17,16},{19,... | collective-permute-start | bytes 294920 | tf_op jit(solution)/shard_map/while/body/eval_jaxpr/ppermute | solution.py:25
  214.8 22.6 %collective-permute-start = (bf16[1,96,512]{2,1,0:T(8,128)(2,1)S(1)}, bf16[1,96,512]{2,1,0:T(8,128)(2,1)S(1)}, u32[]{:S(2)}, u32[]{:S(2)}) collective-permute-start(bf16[1,96,512]{2,1,0:T(8,128)(2,1)S(1)} %add_bitcast_fusion.8), channel_id=1, source_target_pairs={{0,2},{2,4},{4,6},{6,8},{8,10},{10,12},{12,14},{14,16},{16,18},{18... | collective-permute-start | bytes 294920 | tf_op jit(solution)/shard_map/while/body/eval_jaxpr/ppermute | solution.py:22
  232.8 12.0 %collective-permute-start.1 = (bf16[1,96,512]{2,1,0:T(8,128)(2,1)S(1)}, bf16[1,96,512]{2,1,0:T(8,128)(2,1)S(1)}, u32[]{:S(2)}, u32[]{:S(2)}) collective-permute-start(bf16[1,96,512]{2,1,0:T(8,128)(2,1)S(1)} %add_bitcast_fusion.9), channel_id=1, source_target_pairs={{2,0},{4,2},{6,4},{8,6},{10,8},{12,10},{14,12},{16,14},{18,16},{20... | collective-permute-start | bytes 294920 | tf_op jit(solution)/shard_map/while/body/eval_jaxpr/ppermute | solution.py:25
  234.2 10.7 %collective-permute-start.2 = (bf16[1,96,512]{2,1,0:T(8,128)(2,1)S(1)}, bf16[1,96,512]{2,1,0:T(8,128)(2,1)S(1)}, u32[]{:S(2)}, u32[]{:S(2)}) collective-permute-start(bf16[1,96,512]{2,1,0:T(8,128)(2,1)S(1)} %add_bitcast_fusion.10), channel_id=1, source_target_pairs={{0,1},{2,3},{4,5},{6,7},{8,9},{10,11},{12,13},{14,15},{16,17},{18,... | collective-permute-start | bytes 294920 | tf_op jit(solution)/shard_map/while/body/eval_jaxpr/ppermute | solution.py:22
  235.7 9.1 %collective-permute-start.3 = (bf16[1,96,512]{2,1,0:T(8,128)(2,1)S(1)}, bf16[1,96,512]{2,1,0:T(8,128)(2,1)S(1)}, u32[]{:S(2)}, u32[]{:S(2)}) collective-permute-start(bf16[1,96,512]{2,1,0:T(8,128)(2,1)S(1)} %add_bitcast_fusion.11), channel_id=1, source_target_pairs={{1,0},{3,2},{5,4},{7,6},{9,8},{11,10},{13,12},{15,14},{17,16},{19,... | collective-permute-start | bytes 294920 | tf_op jit(solution)/shard_map/while/body/eval_jaxpr/ppermute | solution.py:25
  245.1 19.4 %collective-permute-start = (bf16[1,96,512]{2,1,0:T(8,128)(2,1)S(1)}, bf16[1,96,512]{2,1,0:T(8,128)(2,1)S(1)}, u32[]{:S(2)}, u32[]{:S(2)}) collective-permute-start(bf16[1,96,512]{2,1,0:T(8,128)(2,1)S(1)} %add_bitcast_fusion.8), channel_id=1, source_target_pairs={{0,2},{2,4},{4,6},{6,8},{8,10},{10,12},{12,14},{14,16},{16,18},{18... | collective-permute-start | bytes 294920 | tf_op jit(solution)/shard_map/while/body/eval_jaxpr/ppermute | solution.py:22
  259.8 13.6 %collective-permute-start.1 = (bf16[1,96,512]{2,1,0:T(8,128)(2,1)S(1)}, bf16[1,96,512]{2,1,0:T(8,128)(2,1)S(1)}, u32[]{:S(2)}, u32[]{:S(2)}) collective-permute-start(bf16[1,96,512]{2,1,0:T(8,128)(2,1)S(1)} %add_bitcast_fusion.9), channel_id=1, source_target_pairs={{2,0},{4,2},{6,4},{8,6},{10,8},{12,10},{14,12},{16,14},{18,16},{20... | collective-permute-start | bytes 294920 | tf_op jit(solution)/shard_map/while/body/eval_jaxpr/ppermute | solution.py:25
  261.2 12.3 %collective-permute-start.2 = (bf16[1,96,512]{2,1,0:T(8,128)(2,1)S(1)}, bf16[1,96,512]{2,1,0:T(8,128)(2,1)S(1)}, u32[]{:S(2)}, u32[]{:S(2)}) collective-permute-start(bf16[1,96,512]{2,1,0:T(8,128)(2,1)S(1)} %add_bitcast_fusion.10), channel_id=1, source_target_pairs={{0,1},{2,3},{4,5},{6,7},{8,9},{10,11},{12,13},{14,15},{16,17},{18,... | collective-permute-start | bytes 294920 | tf_op jit(solution)/shard_map/while/body/eval_jaxpr/ppermute | solution.py:22
  262.9 10.6 %collective-permute-start.3 = (bf16[1,96,512]{2,1,0:T(8,128)(2,1)S(1)}, bf16[1,96,512]{2,1,0:T(8,128)(2,1)S(1)}, u32[]{:S(2)}, u32[]{:S(2)}) collective-permute-start(bf16[1,96,512]{2,1,0:T(8,128)(2,1)S(1)} %add_bitcast_fusion.11), channel_id=1, source_target_pairs={{1,0},{3,2},{5,4},{7,6},{9,8},{11,10},{13,12},{15,14},{17,16},{19,... | collective-permute-start | bytes 294920 | tf_op jit(solution)/shard_map/while/body/eval_jaxpr/ppermute | solution.py:25
  273.7 18.0 %collective-permute-start = (bf16[1,96,512]{2,1,0:T(8,128)(2,1)S(1)}, bf16[1,96,512]{2,1,0:T(8,128)(2,1)S(1)}, u32[]{:S(2)}, u32[]{:S(2)}) collective-permute-start(bf16[1,96,512]{2,1,0:T(8,128)(2,1)S(1)} %add_bitcast_fusion.8), channel_id=1, source_target_pairs={{0,2},{2,4},{4,6},{6,8},{8,10},{10,12},{12,14},{14,16},{16,18},{18... | collective-permute-start | bytes 294920 | tf_op jit(solution)/shard_map/while/body/eval_jaxpr/ppermute | solution.py:22
  286.9 9.0 %collective-permute-start.1 = (bf16[1,96,512]{2,1,0:T(8,128)(2,1)S(1)}, bf16[1,96,512]{2,1,0:T(8,128)(2,1)S(1)}, u32[]{:S(2)}, u32[]{:S(2)}) collective-permute-start(bf16[1,96,512]{2,1,0:T(8,128)(2,1)S(1)} %add_bitcast_fusion.9), channel_id=1, source_target_pairs={{2,0},{4,2},{6,4},{8,6},{10,8},{12,10},{14,12},{16,14},{18,16},{20... | collective-permute-start | bytes 294920 | tf_op jit(solution)/shard_map/while/body/eval_jaxpr/ppermute | solution.py:25
  288.2 7.7 %collective-permute-start.2 = (bf16[1,96,512]{2,1,0:T(8,128)(2,1)S(1)}, bf16[1,96,512]{2,1,0:T(8,128)(2,1)S(1)}, u32[]{:S(2)}, u32[]{:S(2)}) collective-permute-start(bf16[1,96,512]{2,1,0:T(8,128)(2,1)S(1)} %add_bitcast_fusion.10), channel_id=1, source_target_pairs={{0,1},{2,3},{4,5},{6,7},{8,9},{10,11},{12,13},{14,15},{16,17},{18,... | collective-permute-start | bytes 294920 | tf_op jit(solution)/shard_map/while/body/eval_jaxpr/ppermute | solution.py:22
  290.0 6.5 %collective-permute-start.3 = (bf16[1,96,512]{2,1,0:T(8,128)(2,1)S(1)}, bf16[1,96,512]{2,1,0:T(8,128)(2,1)S(1)}, u32[]{:S(2)}, u32[]{:S(2)}) collective-permute-start(bf16[1,96,512]{2,1,0:T(8,128)(2,1)S(1)} %add_bitcast_fusion.11), channel_id=1, source_target_pairs={{1,0},{3,2},{5,4},{7,6},{9,8},{11,10},{13,12},{15,14},{17,16},{19,... | collective-permute-start | bytes 294920 | tf_op jit(solution)/shard_map/while/body/eval_jaxpr/ppermute | solution.py:25
  296.8 17.2 %collective-permute-start = (bf16[1,96,512]{2,1,0:T(8,128)(2,1)S(1)}, bf16[1,96,512]{2,1,0:T(8,128)(2,1)S(1)}, u32[]{:S(2)}, u32[]{:S(2)}) collective-permute-start(bf16[1,96,512]{2,1,0:T(8,128)(2,1)S(1)} %add_bitcast_fusion.8), channel_id=1, source_target_pairs={{0,2},{2,4},{4,6},{6,8},{8,10},{10,12},{12,14},{14,16},{16,18},{18... | collective-permute-start | bytes 294920 | tf_op jit(solution)/shard_map/while/body/eval_jaxpr/ppermute | solution.py:22
  309.1 4.9 %collective-permute-start.1 = (bf16[1,96,512]{2,1,0:T(8,128)(2,1)S(1)}, bf16[1,96,512]{2,1,0:T(8,128)(2,1)S(1)}, u32[]{:S(2)}, u32[]{:S(2)}) collective-permute-start(bf16[1,96,512]{2,1,0:T(8,128)(2,1)S(1)} %add_bitcast_fusion.9), channel_id=1, source_target_pairs={{2,0},{4,2},{6,4},{8,6},{10,8},{12,10},{14,12},{16,14},{18,16},{20... | collective-permute-start | bytes 294920 | tf_op jit(solution)/shard_map/while/body/eval_jaxpr/ppermute | solution.py:25
  310.5 4.8 %collective-permute-start.2 = (bf16[1,96,512]{2,1,0:T(8,128)(2,1)S(1)}, bf16[1,96,512]{2,1,0:T(8,128)(2,1)S(1)}, u32[]{:S(2)}, u32[]{:S(2)}) collective-permute-start(bf16[1,96,512]{2,1,0:T(8,128)(2,1)S(1)} %add_bitcast_fusion.10), channel_id=1, source_target_pairs={{0,1},{2,3},{4,5},{6,7},{8,9},{10,11},{12,13},{14,15},{16,17},{18,... | collective-permute-start | bytes 294920 | tf_op jit(solution)/shard_map/while/body/eval_jaxpr/ppermute | solution.py:22
  312.3 7.4 %collective-permute-start.3 = (bf16[1,96,512]{2,1,0:T(8,128)(2,1)S(1)}, bf16[1,96,512]{2,1,0:T(8,128)(2,1)S(1)}, u32[]{:S(2)}, u32[]{:S(2)}) collective-permute-start(bf16[1,96,512]{2,1,0:T(8,128)(2,1)S(1)} %add_bitcast_fusion.11), channel_id=1, source_target_pairs={{1,0},{3,2},{5,4},{7,6},{9,8},{11,10},{13,12},{15,14},{17,16},{19,... | collective-permute-start | bytes 294920 | tf_op jit(solution)/shard_map/while/body/eval_jaxpr/ppermute | solution.py:25
  329.1 6.1 %collective-permute-start.4 = (bf16[1,1,96,512]{3,2,1,0:T(8,128)(2,1)S(1)}, bf16[1,1,96,512]{3,2,1,0:T(8,128)(2,1)S(1)}, u32[]{:S(2)}, u32[]{:S(2)}) collective-permute-start(bf16[1,1,96,512]{3,2,1,0:T(8,128)(2,1)S(1)} %get-tuple-element.571), channel_id=1, source_target_pairs={{0,2},{2,4},{4,6},{6,8},{8,10},{10,12},{12,14},{14,16},{16,18},{18... | collective-permute-start | bytes 294920 | tf_op jit(solution)/shard_map/ppermute | solution.py:22
  333.7 7.6 %collective-permute-start.7 = (bf16[1,1,96,512]{3,2,1,0:T(8,128)(2,1)S(1)}, bf16[1,1,96,512]{3,2,1,0:T(8,128)(2,1)S(1)}, u32[]{:S(2)}, u32[]{:S(2)}) collective-permute-start(bf16[1,1,96,512]{3,2,1,0:T(8,128)(2,1)S(1)} %get-tuple-element.572), channel_id=1, source_target_pairs={{1,0},{3,2},{5,4},{7,6},{9,8},{11,10},{13,12},{15,14},{17,16},{19,... | collective-permute-start | bytes 294920 | tf_op jit(solution)/shard_map/ppermute | solution.py:25
  (13 other events, 84.7 us)
where the time goes:
time: 345 us; the launch traced here: 342 us
  starting transfers between devices  191 us (55%)
  waiting for transfers between devices  99.9 us (29%)
  matrix products  34.5 us (10%)
  other arithmetic  7.32 us (2%)
  loops' own time  5.93 us (2%)
    ppermute x36, starting transfers between devices, padded(): lax.ppermute(lax.slice_in_dim(block, block.shape[dim] - width, None, axis...  145 us
    ppermute x36, waiting for transfers between devices, padded(): lax.ppermute(lax.slice_in_dim(block, 0, width, axis=dim), axis, backward)  94.3 us
    ppermute x36, starting transfers between devices, padded(): lax.ppermute(lax.slice_in_dim(block, 0, width, axis=dim), axis, backward)  46.5 us
    dot_general x8, matrix products, solve_sides(): jnp.dot(row_trace, block_of(in_row, out_side), preferred_element_type=jnp...  10.1 us
    dot_general x8, matrix products, solve_sides(): jnp.dot(col_trace, block_of(in_col, out_side), preferred_element_type=jnp...  10.1 us
  transfers between devices with their start and end apart: 72, of which 32 were waited for; matrix products, arithmetic and copies ran while one was open for 5% of the time, Pallas kernels for 0%

commit v1 on v0

v1 whole, which is shorter than its diff:
```python
import functools

import jax
import jax.numpy as jnp
from jax import lax
from jax.experimental import pallas as pl
from jax.experimental.pallas import tpu as pltpu
from jax.sharding import PartitionSpec as P

MESH = pl.DeviceIdType.MESH


def kernel(
    row_count, col_count, forcing, op, material, stiffness, pre_out, res_out,
    source, half, mat, base, acc, tmp_row, tmp_col, sent, got, rim_sent, rim_got,
    pre, res, classes, load_sem, op_sem, out_sem, sent_sem, got_sem, rim_send_sem, rim_got_sem,
):
    width = base.shape[-1]
    row = lax.axis_index("row")
    col = lax.axis_index("col")

    def columns(side):
        return pl.ds(pl.multiple_of(side * width, width), width)

    low_half = row * 2 < row_count
    order = [jnp.where(low_half, 1, 0), 3, 2, jnp.where(low_half, 0, 1)]
    load_forcing = pltpu.make_async_copy(forcing.at[0, 0], source, load_sem.at[0])
    load_classes = pltpu.make_async_copy(material.at[0], classes, load_sem.at[1])

    def load_op(side):
        return pltpu.make_async_copy(op.at[0, 0, :, columns(side)], mat.at[side], op_sem.at[side])

    load_forcing.start()
    for side in order:
        load_op(side).start()
    load_classes.start()

    below, above = row > 0, row < row_count - 1
    left, right = col > 0, col < col_count - 1
    neighbours = (
        (below, {"row": row - 1}), (above, {"row": row + 1}),
        (left, {"col": col - 1}), (right, {"col": col + 1}),
    )
    barrier = pltpu.get_barrier_semaphore()
    for there, who in neighbours:
        @pl.when(there)
        def _(who=who):
            pl.semaphore_signal(barrier, inc=1, device_id=who, device_id_type=MESH)

    load_forcing.wait()
    half[...] = source[...].astype(jnp.bfloat16)
    acc[...] = jnp.zeros_like(acc)

    for position, side in enumerate(order):
        load_op(side).wait()
        base[side] = jnp.dot(half[...], mat[side], preferred_element_type=jnp.float32)

    count = sum(jnp.where(there, 1, 0) for there, _ in neighbours)
    pl.semaphore_wait(barrier, count)

    ticks = []
    for heading in range(4):
        row_part = row if heading < 2 else row_count - 1 - row
        col_part = col if heading % 2 == 0 else col_count - 1 - col
        ticks.append((row_part + col_part) * 4 + heading)
    ranks = [
        sum(jnp.where(ticks[other] < ticks[mine], 1, 0) for other in range(4) if other != mine)
        for mine in range(4)
    ]

    def trace_copy(heading, kind, who):
        return pltpu.make_async_remote_copy(
            src_ref=sent.at[heading, kind],
            dst_ref=got.at[heading, kind],
            send_sem=sent_sem.at[heading, kind],
            recv_sem=got_sem.at[heading, kind],
            device_id=who,
            device_id_type=MESH,
        )

    def facts(heading):
        back_row, back_col = heading // 2, heading % 2
        to_row, to_col = 1 - 2 * back_row, 1 - 2 * back_col
        next_row, next_col = row + to_row, col + to_col
        last_row, last_col = row - to_row, col - to_col
        has_row = jnp.logical_and(last_row >= 0, last_row < row_count)
        has_col = jnp.logical_and(last_col >= 0, last_col < col_count)
        gives_row = jnp.logical_and(next_row >= 0, next_row < row_count)
        gives_col = jnp.logical_and(next_col >= 0, next_col < col_count)
        return back_row, back_col, next_row, next_col, has_row, has_col, gives_row, gives_col

    def solve(position, carry):
        heading = sum(jnp.where(ranks[h] == position, h, 0) for h in range(4))
        back_row, back_col, next_row, next_col, has_row, has_col, gives_row, gives_col = facts(heading)
        in_row, out_row, in_col, out_col = back_row, 1 - back_row, 2 + back_col, 3 - back_col

        def times(kind, in_side, out_side):
            return jnp.dot(
                got[heading, kind], mat[out_side, columns(in_side), :],
                preferred_element_type=jnp.float32,
            )

        tmp_row[...] = base[out_row]
        tmp_col[...] = base[out_col]

        @pl.when(has_col)
        def _():
            trace_copy(heading, 1, {"col": col}).wait_recv()
            tmp_row[...] += times(1, in_col, out_row)
            tmp_col[...] += times(1, in_col, out_col)

        @pl.when(has_row)
        def _():
            trace_copy(heading, 0, {"row": row}).wait_recv()
            tmp_row[...] += times(0, in_row, out_row)

        @pl.when(gives_row)
        def _():
            sent[heading, 0] = tmp_row[...].astype(jnp.bfloat16)
            trace_copy(heading, 0, {"row": next_row}).start()

        @pl.when(has_row)
        def _():
            tmp_col[...] += times(0, in_row, out_col)

        @pl.when(gives_col)
        def _():
            sent[heading, 1] = tmp_col[...].astype(jnp.bfloat16)
            trace_copy(heading, 1, {"col": next_col}).start()

        acc[out_row] += tmp_row[...]
        acc[out_col] += tmp_col[...]
        acc[in_row] += base[in_row]
        acc[in_col] += base[in_col]

        @pl.when(has_row)
        def _():
            acc[in_row] += times(0, in_row, in_row)
            acc[in_col] += times(0, in_row, in_col)

        @pl.when(has_col)
        def _():
            acc[in_row] += times(1, in_col, in_row)
            acc[in_col] += times(1, in_col, in_col)

        return carry

    lax.fori_loop(0, 4, solve, 0)

    def rim_copy(side, who):
        return pltpu.make_async_remote_copy(
            src_ref=rim_sent.at[side],
            dst_ref=rim_got.at[side ^ 1],
            send_sem=rim_send_sem.at[side],
            recv_sem=rim_got_sem.at[side ^ 1],
            device_id=who,
            device_id_type=MESH,
        )

    def out_copy(kind, side):
        where = pl.ds(side * width, width)
        from_ref, to_ref = ((pre, pre_out), (res, res_out))[kind]
        return pltpu.make_async_copy(
            from_ref.at[side], to_ref.at[0, 0, :, where], out_sem.at[kind, side]
        )

    for side in range(4):
        there, who = neighbours[side]
        value = acc[side] * 0.25
        pre[side] = value
        rim_sent[side] = value.astype(jnp.bfloat16)

        @pl.when(there)
        def _():
            rim_copy(side, who).start()

        @pl.when(jnp.logical_not(there))
        def _():
            rim_got[side] = jnp.zeros_like(rim_got[side])

        out_copy(0, side).start()

    load_classes.wait()
    for side in (0, 1, 2, 3):
        there, who = neighbours[side]
        where = slice(side * width, (side + 1) * width)
        coupling = jnp.zeros((1, width), jnp.float32)
        for index in range(stiffness.shape[0]):
            coupling = coupling + jnp.where(classes[:, where] == index, stiffness[index], 0.0)

        @pl.when(there)
        def _():
            rim_copy(side ^ 1, who).wait_recv()

        value = pre[side]
        facing = rim_got[side].astype(jnp.float32)
        res[side] = source[:, where] - value + coupling * (facing - value)
        out_copy(1, side).start()

    for side in range(4):
        there, who = neighbours[side]

        @pl.when(there)
        def _():
            rim_copy(side, who).wait_send()

        out_copy(0, side).wait()
        out_copy(1, side).wait()
    for heading in range(4):
        _, _, next_row, next_col, _, _, gives_row, gives_col = facts(heading)

        @pl.when(gives_row)
        def _():
            trace_copy(heading, 0, {"row": next_row}).wait_send()

        @pl.when(gives_col)
        def _():
            trace_copy(heading, 1, {"col": next_col}).wait_send()


def local(forcing, local_op, material, stiffness, *, row_count, col_count):
    _, _, loads, order = forcing.shape
    width = order // 4
    side_half = (loads, width)
    any_spec = pl.BlockSpec(memory_space=pl.ANY)
    out = jax.ShapeDtypeStruct(forcing.shape, jnp.float32)
    dma = pltpu.SemaphoreType.DMA
    return pl.pallas_call(
        functools.partial(kernel, row_count, col_count),
        out_shape=(out, out),
        in_specs=[any_spec, any_spec, any_spec, pl.BlockSpec(memory_space=pltpu.SMEM)],
        out_specs=(any_spec, any_spec),
        scratch_shapes=[
            pltpu.VMEM((loads, order), jnp.float32),
            pltpu.VMEM((loads, order), jnp.bfloat16),
            pltpu.VMEM((4, order, width), jnp.bfloat16),
            pltpu.VMEM((4,) + side_half, jnp.float32),
            pltpu.VMEM((4,) + side_half, jnp.float32),
            pltpu.VMEM(side_half, jnp.float32),
            pltpu.VMEM(side_half, jnp.float32),
            pltpu.VMEM((4, 2) + side_half, jnp.bfloat16),
            pltpu.VMEM((4, 2) + side_half, jnp.bfloat16),
            pltpu.VMEM((4,) + side_half, jnp.bfloat16),
            pltpu.VMEM((4,) + side_half, jnp.bfloat16),
            pltpu.VMEM((4,) + side_half, jnp.float32),
            pltpu.VMEM((4,) + side_half, jnp.float32),
            pltpu.VMEM((1, order), jnp.int32),
            dma((2,)),
            dma((4,)),
            dma((2, 4)),
            dma((4, 2)),
            dma((4, 2)),
            dma((4,)),
            dma((4,)),
        ],
        compiler_params=pltpu.CompilerParams(collective_id=0, has_side_effects=True),
    )(forcing, local_op, material, stiffness)


def solution(mesh):
    sizes = dict(mesh.shape)
    return jax.shard_map(
        functools.partial(local, row_count=sizes["row"], col_count=sizes["col"]),
        mesh=mesh,
        in_specs=(
            P("row", "col", None, None),
            P("row", "col", None, None),
            P("row", "col", None),
            P(),
        ),
        out_specs=(P("row", "col", None, None), P("row", "col", None, None)),
        check_vma=False,
    )
```

time: 345 us -> 59.9 us (0.17)
  starting transfers between devices: 191 us -> 0 us
  waiting for transfers between devices: 99.9 us -> 0 us
  Pallas kernels: 0 us -> 54.9 us
  matrix products: 34.5 us -> 0 us
  other arithmetic: 7.32 us -> 0 us
  loops' own time: 5.93 us -> 0 us
    ppermute x72 -> x0, starting transfers between devices: 191 us -> none  [the longest x36 145 us: padded(): lax.ppermute(lax.slice_in_dim(block, block.shape[dim] - width, None, axis...]
    ppermute x72 -> x0, waiting for transfers between devices: 99.9 us -> none  [the longest x36 94.3 us: padded(): lax.ppermute(lax.slice_in_dim(block, 0, width, axis=dim), axis, backward)]
    pallas_call x0 -> x1, Pallas kernels: none -> 54.9 us  [local(): pl.pallas_call(functools.partial(kernel, row_count, col_count), out_shape...]
    dot_general x25 -> x0, matrix products: 34.5 us -> none  [the longest x8 10.1 us: solve_sides(): jnp.dot(row_trace, block_of(in_row, out_side), preferred_element_type=jnp...]
    another operation x69 -> x0, loops' own time: 5.93 us -> none  [the longest x1 4.07 us: local(): lax.fori_loop(0, tick_count, tick_step, start_state)]
    select_n x68 -> x0, other arithmetic: 5.25 us -> none  [the longest x34 2.63 us: tick_step(): jnp.where(active, col_traces[heading_index], kept_cols[heading_index])]
    unnamed x10 -> x2, local copies, waits for them, and re-layouts: 0.03 us -> 4.13 us
  transfers between devices with their start and end apart: 72 -> 0, of which waited for: 32 -> 0; matrix products, arithmetic and copies ran while one was open for 5% -> 0% of each run, Pallas kernels for 0% -> 0%
where the time goes in v1:
time: 59.9 us; the launch traced here: 59.7 us
  Pallas kernels  54.9 us (92%)
  local copies, waits for them, and re-layouts  4.13 us (7%)
  between operations  0.64 us (1%)
    pallas_call x1, Pallas kernels, local(): pl.pallas_call(functools.partial(kernel, row_count, col_count), out_shape...  54.9 us
    unnamed x2, local copies, waits for them, and re-layouts  4.13 us

profile of v1, /device:TPU:0, one launch (start us, length us, event | category | flops | bytes accessed | tf_op | source)
XLA Modules:
  0.0 59.7 jit_solution(12355075586486635852)
XLA Ops:
  0.6 54.9 %shard_map.59 = (f32[1,1,96,2048]{3,2,1,0:T(8,128)}, f32[1,1,96,2048]{3,2,1,0:T(8,128)}) custom-call(f32[1,1,96,2048]{3,2,1,0:T(8,128)} %forcing.1, bf16[1,1,2048,2048]{3,2,1,0:T(8,128)(2,1)} %op.1, s32[1,1,2048]{2,1,0:T(1,128)} %material.1, f32[8]{0:T(128)} %stiffness.1), custom_call_target="tpu_custom_call" | custom-call | tf_op jit(solution)/shard_map/pallas_call | solution.py:228
  55.6 2.1 %copy.8 = f32[1,1,96,2048]{3,2,1,0:T(8,128)} copy(f32[1,1,96,2048]{3,2,1,0:T(8,128)} %get-tuple-element.4) | data formatting | bytes 1572864
  57.6 2.1 %copy.9 = f32[1,1,96,2048]{3,2,1,0:T(8,128)} copy(f32[1,1,96,2048]{3,2,1,0:T(8,128)} %get-tuple-element.5) | data formatting | bytes 1572864

commit v2 on v1

v2 whole, which is shorter than its diff:
```python
import functools

import jax
import jax.numpy as jnp
from jax import lax
from jax.experimental import pallas as pl
from jax.experimental.pallas import tpu as pltpu
from jax.sharding import PartitionSpec as P

MESH = pl.DeviceIdType.MESH


def kernel(
    row_count, col_count, forcing, op, material, stiffness, sum_out, facing_out, coupling_out,
    source, half, mat, base, acc, tmp_row, tmp_col, twin_mat, twin_base, cross,
    row_sent, row_got, col_sent, col_got, twin_row, twin_col, rim_sent, rim_got, coupling, classes,
    load_sem, op_sem, out_sem, mat_sem, base_sem, row_sem, col_sem, cross_sem, relay_sem, rim_sem,
):
    width = base.shape[-1]
    row = lax.axis_index("row")
    col = lax.axis_index("col")
    core = row % 2
    pair = row // 2
    pair_count = row_count // 2
    step = 1 - 2 * core
    twin = row + step
    in_row, out_row = core, 1 - core
    left, right = col > 0, col < col_count - 1
    has_row = jnp.where(core == 0, pair, pair_count - 1 - pair) > 0
    gives_row = jnp.where(core == 0, pair_count - 1 - pair, pair) > 0

    def columns(side):
        return pl.ds(pl.multiple_of(side * width, width), width)

    def remote(src, dst, sem, place, who):
        return pltpu.make_async_remote_copy(
            src_ref=src, dst_ref=dst, send_sem=sem.at[(0,) + place], recv_sem=sem.at[(1,) + place],
            device_id=who, device_id_type=MESH,
        )

    def dot(left_value, right_value):
        return jnp.dot(left_value, right_value, preferred_element_type=jnp.float32)

    first = jnp.where(col <= col_count - 1 - col, 0, 1)
    low_half = pair * 2 < pair_count
    order = [jnp.where(low_half, 1, 0), 3 - first, 2 + first, jnp.where(low_half, 0, 1)]
    load_forcing = pltpu.make_async_copy(forcing.at[0, 0], source, load_sem.at[0])
    load_classes = pltpu.make_async_copy(material.at[0], classes, load_sem.at[1])

    def load_op(side):
        return pltpu.make_async_copy(op.at[0, 0, :, columns(side)], mat.at[side], op_sem.at[side])

    load_forcing.start()
    for side in order:
        load_op(side).start()
    load_classes.start()

    partners = (
        (row > 0, {"row": row - 1}), (row < row_count - 1, {"row": row + 1}),
        (row > 1, {"row": row - 2}), (row < row_count - 2, {"row": row + 2}),
        (left, {"col": col - 1}), (right, {"col": col + 1}),
    )
    neighbours = (partners[0], partners[1], partners[4], partners[5])
    barrier = pltpu.get_barrier_semaphore()
    for there, who in partners:
        @pl.when(there)
        def _(who=who):
            pl.semaphore_signal(barrier, inc=1, device_id=who, device_id_type=MESH)
    pl.semaphore_wait(barrier, sum(jnp.where(there, 1, 0) for there, _ in partners))

    def has_col(d):
        return jnp.where(d == 0, col, col_count - 1 - col) > 0

    def gives_col(d):
        return jnp.where(d == 0, col_count - 1 - col, col) > 0

    def mat_copy(slot, in_side, out_side):
        return remote(
            op.at[0, 0, columns(in_side), columns(out_side)], twin_mat.at[slot], mat_sem, (slot,),
            {"row": twin},
        )

    twin_in, twin_out = 1 - core, core
    shared = [(row >= 0, 0, twin_in, twin_out)]
    for d in (0, 1):
        enters, leaves = has_col(d), gives_col(d)
        shared.append((leaves, 1 + 3 * d, twin_in, 3 - d))
        shared.append((enters, 2 + 3 * d, 2 + d, twin_out))
        shared.append((jnp.logical_and(enters, leaves), 3 + 3 * d, 2 + d, 3 - d))

    def all_shared(act):
        for there, slot, in_side, out_side in shared:
            @pl.when(there)
            def _(slot=slot, in_side=in_side, out_side=out_side):
                act(mat_copy(slot, in_side, out_side))

    all_shared(lambda copy: copy.start())

    def base_copy(slot, side):
        return remote(base.at[side], twin_base.at[slot], base_sem, (slot,), {"row": twin})

    load_forcing.wait()
    half[...] = source[...].astype(jnp.bfloat16)

    def make_base(side):
        load_op(side).wait()
        base[side] = dot(half[...], mat[side])

        @pl.when(side == twin_out)
        def _():
            base_copy(0, side).start()

        for d in (0, 1):
            @pl.when(jnp.logical_and(side == 3 - d, gives_col(d)))
            def _(d=d):
                base_copy(1 + d, side).start()

    def row_copy(d):
        return remote(
            row_sent.at[d], row_got.at[d], row_sem, (d,), {"row": row + 2 * step}
        )

    def col_copy(d, cell):
        return remote(
            col_sent.at[d, cell], col_got.at[d, cell], col_sem, (d, cell), {"col": col + 1 - 2 * d}
        )

    def cross_copy(d):
        return remote(cross.at[d], twin_row.at[d], cross_sem, (d,), {"row": twin})

    def relay_copy(d):
        return remote(col_got.at[d, 1], twin_col.at[d], relay_sem, (d,), {"row": twin})

    def solve(d, wait_shared):
        in_col, out_col = 2 + d, 3 - d
        enters, leaves = has_col(d), gives_col(d)
        tmp_row[0] = base[out_row]

        if wait_shared:
            base_copy(0, out_row).wait_recv()
            mat_copy(0, twin_in, twin_out).wait_recv()
        tmp_row[1] = twin_base[0]

        @pl.when(enters)
        def _():
            col_copy(d, 0).wait_recv()
            tmp_row[0] += dot(col_got[d, 0], mat[out_row, columns(in_col), :])
            mat_copy(2 + 3 * d, 0, 0).wait_recv()
            col_copy(d, 1).wait_recv()
            relay_copy(d).start()
            tmp_row[1] += dot(col_got[d, 1], twin_mat[2 + 3 * d])

        @pl.when(has_row)
        def _():
            row_copy(d).wait_recv()
            tmp_row[0] += dot(row_got[d], mat[out_row, columns(in_row), :])

        cross[d] = tmp_row[0].astype(jnp.bfloat16)

        @pl.when(gives_row)
        def _():
            row_sent[d] = (tmp_row[1] + dot(cross[d], twin_mat[0])).astype(jnp.bfloat16)
            row_copy(d).start()

        @pl.when(leaves)
        def _():
            tmp_col[...] = base[out_col]

            @pl.when(enters)
            def _():
                tmp_col[...] += dot(col_got[d, 0], mat[out_col, columns(in_col), :])

            @pl.when(has_row)
            def _():
                tmp_col[...] += dot(row_got[d], mat[out_col, columns(in_row), :])

            col_sent[d, 0] = tmp_col[...].astype(jnp.bfloat16)
            col_copy(d, 0).start()
            base_copy(1 + d, 0).wait_recv()
            mat_copy(1 + 3 * d, 0, 0).wait_recv()
            tmp_col[...] = twin_base[1 + d] + dot(cross[d], twin_mat[1 + 3 * d])

            @pl.when(enters)
            def _():
                mat_copy(3 + 3 * d, 0, 0).wait_recv()
                tmp_col[...] += dot(col_got[d, 1], twin_mat[3 + 3 * d])

            col_sent[d, 1] = tmp_col[...].astype(jnp.bfloat16)
            col_copy(d, 1).start()

        cross_copy(d).start()

    def add_terms(trace, in_side):
        def one(side, carry):
            acc[side] += dot(trace[...], mat[side, columns(in_side), :])
            return carry

        lax.fori_loop(0, 4, one, 0)

    def own_terms(d):
        @pl.when(has_row)
        def _():
            add_terms(row_got.at[d], in_row)

        @pl.when(has_col(d))
        def _():
            add_terms(col_got.at[d, 0], 2 + d)

    def twin_terms():
        def one(position, carry):
            d = jnp.where(position == 0, first, 1 - first)
            cross_copy(d).wait_recv()
            add_terms(twin_row.at[d], 1 - core)

            @pl.when(has_col(d))
            def _():
                relay_copy(d).wait_recv()
                add_terms(twin_col.at[d], 2 + d)

            return carry

        lax.fori_loop(0, 2, one, 0)

    make_base(order[0])
    make_base(order[1])
    early = jnp.logical_and(
        jnp.where(low_half, 0, 1) == core,
        jnp.logical_not(jnp.logical_or(has_row, has_col(first))),
    )

    @pl.when(early)
    def _():
        solve(first, True)

    make_base(order[2])
    make_base(order[3])
    acc[...] = base[...] * 4.0

    depth = jnp.where(core == 0, pair, pair_count - 1 - pair)
    twin_first = depth * 2 >= pair_count + 2

    @pl.when(twin_first)
    def _():
        twin_terms()

    @pl.when(jnp.logical_not(early))
    def _():
        solve(first, True)

    own_terms(first)
    solve(1 - first, False)
    own_terms(1 - first)

    @pl.when(jnp.logical_not(twin_first))
    def _():
        twin_terms()

    def rim_copy(side, who):
        return pltpu.make_async_remote_copy(
            src_ref=rim_sent.at[side], dst_ref=rim_got.at[side ^ 1],
            send_sem=rim_sem.at[0, side], recv_sem=rim_sem.at[1, side ^ 1],
            device_id=who, device_id_type=MESH,
        )

    def out_copy(kind, side):
        where = pl.ds(side * width, width)
        from_ref, to_ref = ((acc, sum_out), (rim_got, facing_out))[kind]
        return pltpu.make_async_copy(
            from_ref.at[side], to_ref.at[0, 0, :, where], out_sem.at[kind, side]
        )

    for side in range(4):
        there, who = neighbours[side]
        rim_sent[side] = (acc[side] * 0.25).astype(jnp.bfloat16)

        @pl.when(there)
        def _():
            rim_copy(side, who).start()

        @pl.when(jnp.logical_not(there))
        def _():
            rim_got[side] = jnp.zeros_like(rim_got[side])

        out_copy(0, side).start()

    load_classes.wait()
    total = jnp.zeros(coupling.shape, jnp.float32)
    for index in range(stiffness.shape[0]):
        total = total + jnp.where(classes[...] == index, stiffness[index], 0.0)
    coupling[...] = total
    coupling_copy = pltpu.make_async_copy(coupling, coupling_out.at[0], load_sem.at[2])
    coupling_copy.start()

    for side in range(4):
        there, who = neighbours[side]

        @pl.when(there)
        def _():
            rim_copy(side ^ 1, who).wait_recv()

        out_copy(1, side).start()

    for side in range(4):
        there, who = neighbours[side]

        @pl.when(there)
        def _():
            rim_copy(side, who).wait_send()

        out_copy(0, side).wait()
        out_copy(1, side).wait()
    coupling_copy.wait()
    all_shared(lambda copy: copy.wait_send())
    base_copy(0, 0).wait_send()
    for d in (0, 1):
        cross_copy(d).wait_send()

        @pl.when(gives_row)
        def _():
            row_copy(d).wait_send()

        @pl.when(has_col(d))
        def _():
            relay_copy(d).wait_send()

        @pl.when(gives_col(d))
        def _():
            base_copy(1 + d, 0).wait_send()
            col_copy(d, 0).wait_send()
            col_copy(d, 1).wait_send()


def local(forcing, local_op, material, stiffness, *, row_count, col_count):
    _, _, loads, order = forcing.shape
    width = order // 4
    side = (loads, width)
    any_spec = pl.BlockSpec(memory_space=pl.ANY)
    dma = pltpu.SemaphoreType.DMA
    f32, b16 = jnp.float32, jnp.bfloat16
    summed, facing, coupling = pl.pallas_call(
        functools.partial(kernel, row_count, col_count),
        out_shape=(
            jax.ShapeDtypeStruct(forcing.shape, f32),
            jax.ShapeDtypeStruct(forcing.shape, b16),
            jax.ShapeDtypeStruct(material.shape, f32),
        ),
        in_specs=[any_spec, any_spec, any_spec, pl.BlockSpec(memory_space=pltpu.SMEM)],
        out_specs=(any_spec,) * 3,
        scratch_shapes=[
            pltpu.VMEM((loads, order), f32),
            pltpu.VMEM((loads, order), b16),
            pltpu.VMEM((4, order, width), b16),
            pltpu.VMEM((4,) + side, f32),
            pltpu.VMEM((4,) + side, f32),
            pltpu.VMEM((2,) + side, f32),
            pltpu.VMEM(side, f32),
            pltpu.VMEM((7, width, width), b16),
            pltpu.VMEM((3,) + side, f32),
            pltpu.VMEM((2,) + side, b16),
            pltpu.VMEM((2,) + side, b16),
            pltpu.VMEM((2,) + side, b16),
            pltpu.VMEM((2, 2) + side, b16),
            pltpu.VMEM((2, 2) + side, b16),
            pltpu.VMEM((2,) + side, b16),
            pltpu.VMEM((2,) + side, b16),
            pltpu.VMEM((4,) + side, b16),
            pltpu.VMEM((4,) + side, b16),
            pltpu.VMEM((1, order), f32),
            pltpu.VMEM((1, order), jnp.int32),
            dma((3,)),
            dma((4,)),
            dma((2, 4)),
            dma((2, 7)),
            dma((2, 3)),
            dma((2, 2)),
            dma((2, 2, 2)),
            dma((2, 2)),
            dma((2, 2)),
            dma((2, 4)),
        ],
        compiler_params=pltpu.CompilerParams(collective_id=0, has_side_effects=True),
    )(forcing, local_op, material, stiffness)
    preconditioned = summed * 0.25
    gap = facing.astype(f32) - preconditioned
    residual = forcing - preconditioned + coupling[:, :, None, :] * gap
    return preconditioned, residual


def solution(mesh):
    sizes = dict(mesh.shape)
    return jax.shard_map(
        functools.partial(local, row_count=sizes["row"], col_count=sizes["col"]),
        mesh=mesh,
        in_specs=(
            P("row", "col", None, None),
            P("row", "col", None, None),
            P("row", "col", None),
            P(),
        ),
        out_specs=(P("row", "col", None, None), P("row", "col", None, None)),
        check_vma=False,
    )
```

time: 59.9 us -> 50.4 us (0.84)
  the two profiles are of different devices: /device:TPU:0 before, /device:TPU:31 now
where the time goes in v2:
time: 50.4 us; the launch traced here: 50.3 us
  Pallas kernels  47 us (93%)
  other arithmetic  2.6 us (5%)
  between operations  0.65 us (1%)
    pallas_call x1, Pallas kernels, local(): pl.pallas_call(functools.partial(kernel, row_count, col_count), out_shape...  47 us
    add x1, other arithmetic, local(): residual = forcing - preconditioned + coupling[:, :, None, :] * gap  2.6 us

profile of v2, /device:TPU:31, one launch (start us, length us, event | category | flops | bytes accessed | tf_op | source)
XLA Modules:
  0.0 50.3 jit_solution(5879112644303486444)
XLA Ops:
  0.6 0.0 copy-start
  0.6 47.0 %shard_map.59 = (f32[1,1,96,2048]{3,2,1,0:T(8,128)}, bf16[1,1,96,2048]{3,2,1,0:T(8,128)(2,1)}, f32[1,1,2048]{2,1,0:T(1,128)}) custom-call(f32[1,1,96,2048]{3,2,1,0:T(8,128)} %forcing.1, bf16[1,1,2048,2048]{3,2,1,0:T(8,128)(2,1)} %op.1, s32[1,1,2048]{2,1,0:T(1,128)} %material.1, f32[8]{0:T(128)} %stiffness.1), custom_call_target="tpu_custom_call" | custom-call | tf_op jit(solution)/shard_map/pallas_call | solution.py:340
  47.7 0.0 copy-done
  47.7 2.6 %multiply_add_fusion = (f32[1,1,96,2048]{3,2,1,0:T(8,128)}, f32[1,1,96,2048]{3,2,1,0:T(8,128)}) fusion(bf16[1,1,96,2048]{3,2,1,0:T(8,128)(2,1)} %get-tuple-element.7, f32[1,1,96,2048]{3,2,1,0:T(8,128)S(1)} %copy-done, f32[2048]{0:T(1024)} %bitcast.1, f32[1,1,96,2048]{3,2,1,0:T(8,128)} %get-tuple-element.5), kind=kLoop, calls=%fused_computation | loop fusion | flops 1179648 | bytes 3547136 | tf_op jit(solution)/shard_map/add | solution.py:385
Async XLA Ops:
  0.6 47.0 %copy-start = (f32[1,1,96,2048]{3,2,1,0:T(8,128)S(1)}, f32[1,1,96,2048]{3,2,1,0:T(8,128)}, u32[]{:S(2)}) copy-start(f32[1,1,96,2048]{3,2,1,0:T(8,128)} %forcing.1) | copy-start | bytes 2359300

commit v3 on v2

--- a/solution.py
+++ b/solution.py
@@ -17,6 +17,8 @@
     load_sem, op_sem, out_sem, mat_sem, base_sem, row_sem, col_sem, cross_sem, relay_sem, rim_sem,
 ):
     width = base.shape[-1]
+    chunks = row_sem.shape[-1]
+    span = base.shape[1] // chunks
     row = lax.axis_index("row")
     col = lax.axis_index("col")
     core = row % 2
@@ -115,9 +117,10 @@
             def _(d=d):
                 base_copy(1 + d, side).start()
 
-    def row_copy(d):
+    def row_copy(d, chunk):
+        part = pl.ds(chunk * span, span)
         return remote(
-            row_sent.at[d], row_got.at[d], row_sem, (d,), {"row": row + 2 * step}
+            row_sent.at[d, part], row_got.at[d, part], row_sem, (d, chunk), {"row": row + 2 * step}
         )
 
     def col_copy(d, cell):
@@ -150,17 +153,28 @@
             relay_copy(d).start()
             tmp_row[1] += dot(col_got[d, 1], twin_mat[2 + 3 * d])
 
-        @pl.when(has_row)
-        def _():
-            row_copy(d).wait_recv()
-            tmp_row[0] += dot(row_got[d], mat[out_row, columns(in_row), :])
-
-        cross[d] = tmp_row[0].astype(jnp.bfloat16)
-
-        @pl.when(gives_row)
-        def _():
-            row_sent[d] = (tmp_row[1] + dot(cross[d], twin_mat[0])).astype(jnp.bfloat16)
-            row_copy(d).start()
+        for chunk in range(chunks):
+            part = pl.ds(chunk * span, span)
+
+            @pl.when(has_row)
+            def _():
+                row_copy(d, chunk).wait_recv()
+                cross[d, part] = (
+                    tmp_row[0, part] + dot(row_got[d, part], mat[out_row, columns(in_row), :])
+                ).astype(jnp.bfloat16)
+
+            @pl.when(jnp.logical_not(has_row))
+            def _():
+                cross[d, part] = tmp_row[0, part].astype(jnp.bfloat16)
+
+            @pl.when(gives_row)
+            def _():
+                row_sent[d, part] = (
+                    tmp_row[1, part] + dot(cross[d, part], twin_mat[0])
+                ).astype(jnp.bfloat16)
+                row_copy(d, chunk).start()
+
+        cross_copy(d).start()
 
         @pl.when(leaves)
         def _():
@@ -188,14 +202,9 @@
             col_sent[d, 1] = tmp_col[...].astype(jnp.bfloat16)
             col_copy(d, 1).start()
 
-        cross_copy(d).start()
-
     def add_terms(trace, in_side):
-        def one(side, carry):
+        for side in range(4):
             acc[side] += dot(trace[...], mat[side, columns(in_side), :])
-            return carry
-
-        lax.fori_loop(0, 4, one, 0)
 
     def own_terms(d):
         @pl.when(has_row)
@@ -317,7 +326,8 @@
 
         @pl.when(gives_row)
         def _():
-            row_copy(d).wait_send()
+            for chunk in range(chunks):
+                row_copy(d, chunk).wait_send()
 
         @pl.when(has_col(d))
         def _():
@@ -334,6 +344,7 @@
     _, _, loads, order = forcing.shape
     width = order // 4
     side = (loads, width)
+    chunks = 2 if loads % 32 == 0 else 1
     any_spec = pl.BlockSpec(memory_space=pl.ANY)
     dma = pltpu.SemaphoreType.DMA
     f32, b16 = jnp.float32, jnp.bfloat16
@@ -372,7 +383,7 @@
             dma((2, 4)),
             dma((2, 7)),
             dma((2, 3)),
-            dma((2, 2)),
+            dma((2, 2, chunks)),
             dma((2, 2, 2)),
             dma((2, 2)),
             dma((2, 2)),

time: 50.4 us -> 47.2 us (0.937)
  Pallas kernels: 47 us -> 43.7 us
    pallas_call x1, Pallas kernels: 47 us -> 43.7 us  [local(): pl.pallas_call(functools.partial(kernel, row_count, col_count), out_shape...]
where the time goes in v3:
time: 47.2 us; the launch traced here: 47 us
  Pallas kernels  43.7 us (93%)
  other arithmetic  2.6 us (6%)
  between operations  0.65 us (1%)
    pallas_call x1, Pallas kernels, local(): pl.pallas_call(functools.partial(kernel, row_count, col_count), out_shape...  43.7 us
    add x1, other arithmetic, local(): residual = forcing - preconditioned + coupling[:, :, None, :] * gap  2.6 us

profile of v3, /device:TPU:31, one launch (start us, length us, event | category | flops | bytes accessed | tf_op | source)
XLA Modules:
  0.0 47.0 jit_solution(8158282136896392448)
XLA Ops:
  0.6 0.0 copy-start
  0.6 43.7 %shard_map.59 = (f32[1,1,96,2048]{3,2,1,0:T(8,128)}, bf16[1,1,96,2048]{3,2,1,0:T(8,128)(2,1)}, f32[1,1,2048]{2,1,0:T(1,128)}) custom-call(f32[1,1,96,2048]{3,2,1,0:T(8,128)} %forcing.1, bf16[1,1,2048,2048]{3,2,1,0:T(8,128)(2,1)} %op.1, s32[1,1,2048]{2,1,0:T(1,128)} %material.1, f32[8]{0:T(128)} %stiffness.1), custom_call_target="tpu_custom_call" | custom-call | tf_op jit(solution)/shard_map/pallas_call | solution.py:351
  44.4 0.0 copy-done
  44.4 2.6 %multiply_add_fusion = (f32[1,1,96,2048]{3,2,1,0:T(8,128)}, f32[1,1,96,2048]{3,2,1,0:T(8,128)}) fusion(bf16[1,1,96,2048]{3,2,1,0:T(8,128)(2,1)} %get-tuple-element.7, f32[1,1,96,2048]{3,2,1,0:T(8,128)S(1)} %copy-done, f32[2048]{0:T(1024)} %bitcast.1, f32[1,1,96,2048]{3,2,1,0:T(8,128)} %get-tuple-element.5), kind=kLoop, calls=%fused_computation | loop fusion | flops 1179648 | bytes 3547136 | tf_op jit(solution)/shard_map/add | solution.py:396
Async XLA Ops:
  0.6 43.8 %copy-start = (f32[1,1,96,2048]{3,2,1,0:T(8,128)S(1)}, f32[1,1,96,2048]{3,2,1,0:T(8,128)}, u32[]{:S(2)}) copy-start(f32[1,1,96,2048]{3,2,1,0:T(8,128)} %forcing.1) | copy-start | bytes 2359300

commit v4 on v3

--- a/solution.py
+++ b/solution.py
@@ -12,7 +12,7 @@
 
 def kernel(
     row_count, col_count, forcing, op, material, stiffness, sum_out, facing_out, coupling_out,
-    source, half, mat, base, acc, tmp_row, tmp_col, twin_mat, twin_base, cross,
+    source, half, mat, base, acc, tmp_row, tmp_col, twin_mat, twin_base, hop, cross,
     row_sent, row_got, col_sent, col_got, twin_row, twin_col, rim_sent, rim_got, coupling, classes,
     load_sem, op_sem, out_sem, mat_sem, base_sem, row_sem, col_sem, cross_sem, relay_sem, rim_sem,
 ):
@@ -134,20 +134,27 @@
     def relay_copy(d):
         return remote(col_got.at[d, 1], twin_col.at[d], relay_sem, (d,), {"row": twin})
 
-    def solve(d, wait_shared):
-        in_col, out_col = 2 + d, 3 - d
-        enters, leaves = has_col(d), gives_col(d)
+    def wait_shared():
+        base_copy(0, 0).wait_recv()
+        mat_copy(0, 0, 0).wait_recv()
+
+    def solve_row(d):
+        in_col = 2 + d
+        enters = has_col(d)
         tmp_row[0] = base[out_row]
-
-        if wait_shared:
-            base_copy(0, out_row).wait_recv()
-            mat_copy(0, twin_in, twin_out).wait_recv()
         tmp_row[1] = twin_base[0]
 
         @pl.when(enters)
         def _():
             col_copy(d, 0).wait_recv()
             tmp_row[0] += dot(col_got[d, 0], mat[out_row, columns(in_col), :])
+
+        @pl.when(gives_row)
+        def _():
+            tmp_row[1] += dot(tmp_row[0].astype(jnp.bfloat16), twin_mat[0])
+
+        @pl.when(enters)
+        def _():
             mat_copy(2 + 3 * d, 0, 0).wait_recv()
             col_copy(d, 1).wait_recv()
             relay_copy(d).start()
@@ -159,22 +166,29 @@
             @pl.when(has_row)
             def _():
                 row_copy(d, chunk).wait_recv()
-                cross[d, part] = (
-                    tmp_row[0, part] + dot(row_got[d, part], mat[out_row, columns(in_row), :])
-                ).astype(jnp.bfloat16)
-
-            @pl.when(jnp.logical_not(has_row))
-            def _():
-                cross[d, part] = tmp_row[0, part].astype(jnp.bfloat16)
-
-            @pl.when(gives_row)
+
+            @pl.when(jnp.logical_and(has_row, gives_row))
             def _():
                 row_sent[d, part] = (
-                    tmp_row[1, part] + dot(cross[d, part], twin_mat[0])
+                    tmp_row[1, part] + dot(row_got[d, part], hop[...])
                 ).astype(jnp.bfloat16)
                 row_copy(d, chunk).start()
 
+            @pl.when(jnp.logical_and(jnp.logical_not(has_row), gives_row))
+            def _():
+                row_sent[d, part] = tmp_row[1, part].astype(jnp.bfloat16)
+                row_copy(d, chunk).start()
+
+        @pl.when(has_row)
+        def _():
+            tmp_row[0] += dot(row_got[d], mat[out_row, columns(in_row), :])
+
+        cross[d] = tmp_row[0].astype(jnp.bfloat16)
         cross_copy(d).start()
+
+    def solve_col(d):
+        in_col, out_col = 2 + d, 3 - d
+        enters, leaves = has_col(d), gives_col(d)
 
         @pl.when(leaves)
         def _():
@@ -230,21 +244,35 @@
 
         lax.fori_loop(0, 2, one, 0)
 
-    make_base(order[0])
-    make_base(order[1])
     early = jnp.logical_and(
         jnp.where(low_half, 0, 1) == core,
         jnp.logical_not(jnp.logical_or(has_row, has_col(first))),
     )
+    make_base(order[0])
 
     @pl.when(early)
     def _():
-        solve(first, True)
+        wait_shared()
+        solve_row(first)
+
+    make_base(order[1])
+
+    @pl.when(early)
+    def _():
+        solve_col(first)
 
     make_base(order[2])
     make_base(order[3])
     acc[...] = base[...] * 4.0
 
+    @pl.when(jnp.logical_not(early))
+    def _():
+        wait_shared()
+
+    @pl.when(jnp.logical_and(has_row, gives_row))
+    def _():
+        hop[...] = dot(mat[out_row, columns(in_row), :], twin_mat[0]).astype(jnp.bfloat16)
+
     depth = jnp.where(core == 0, pair, pair_count - 1 - pair)
     twin_first = depth * 2 >= pair_count + 2
 
@@ -254,10 +282,12 @@
 
     @pl.when(jnp.logical_not(early))
     def _():
-        solve(first, True)
+        solve_row(first)
+        solve_col(first)
 
     own_terms(first)
-    solve(1 - first, False)
+    solve_row(1 - first)
+    solve_col(1 - first)
     own_terms(1 - first)
 
     @pl.when(jnp.logical_not(twin_first))
@@ -367,6 +397,7 @@
             pltpu.VMEM(side, f32),
             pltpu.VMEM((7, width, width), b16),
             pltpu.VMEM((3,) + side, f32),
+            pltpu.VMEM((width, width), b16),
             pltpu.VMEM((2,) + side, b16),
             pltpu.VMEM((2,) + side, b16),
             pltpu.VMEM((2,) + side, b16),

time: 47.2 us -> 46.2 us (0.979)
  Pallas kernels: 43.7 us -> 42.8 us
    pallas_call x1, Pallas kernels: 43.7 us -> 42.8 us  [local(): pl.pallas_call(functools.partial(kernel, row_count, col_count), out_shape...]
where the time goes in v4:
time: 46.2 us; the launch traced here: 46.1 us
  Pallas kernels  42.8 us (93%)
  other arithmetic  2.6 us (6%)
  between operations  0.65 us (1%)
    pallas_call x1, Pallas kernels, local(): pl.pallas_call(functools.partial(kernel, row_count, col_count), out_shape...  42.8 us
    add x1, other arithmetic, local(): residual = forcing - preconditioned + coupling[:, :, None, :] * gap  2.6 us

profile of v4, /device:TPU:31, one launch (start us, length us, event | category | flops | bytes accessed | tf_op | source)
XLA Modules:
  0.0 46.1 jit_solution(7441733024352508131)
XLA Ops:
  0.6 0.0 copy-start
  0.6 42.8 %shard_map.59 = (f32[1,1,96,2048]{3,2,1,0:T(8,128)}, bf16[1,1,96,2048]{3,2,1,0:T(8,128)(2,1)}, f32[1,1,2048]{2,1,0:T(1,128)}) custom-call(f32[1,1,96,2048]{3,2,1,0:T(8,128)} %forcing.1, bf16[1,1,2048,2048]{3,2,1,0:T(8,128)(2,1)} %op.1, s32[1,1,2048]{2,1,0:T(1,128)} %material.1, f32[8]{0:T(128)} %stiffness.1), custom_call_target="tpu_custom_call" | custom-call | tf_op jit(solution)/shard_map/pallas_call | solution.py:381
  43.5 0.0 copy-done
  43.5 2.6 %multiply_add_fusion = (f32[1,1,96,2048]{3,2,1,0:T(8,128)}, f32[1,1,96,2048]{3,2,1,0:T(8,128)}) fusion(bf16[1,1,96,2048]{3,2,1,0:T(8,128)(2,1)} %get-tuple-element.7, f32[1,1,96,2048]{3,2,1,0:T(8,128)S(1)} %copy-done, f32[2048]{0:T(1024)} %bitcast.1, f32[1,1,96,2048]{3,2,1,0:T(8,128)} %get-tuple-element.5), kind=kLoop, calls=%fused_computation | loop fusion | flops 1179648 | bytes 3547136 | tf_op jit(solution)/shard_map/add | solution.py:427
Async XLA Ops:
  0.6 42.8 %copy-start = (f32[1,1,96,2048]{3,2,1,0:T(8,128)S(1)}, f32[1,1,96,2048]{3,2,1,0:T(8,128)}, u32[]{:S(2)}) copy-start(f32[1,1,96,2048]{3,2,1,0:T(8,128)} %forcing.1) | copy-start | bytes 2359300

commit v5 on v4

--- a/solution.py
+++ b/solution.py
@@ -53,9 +53,7 @@
         return pltpu.make_async_copy(op.at[0, 0, :, columns(side)], mat.at[side], op_sem.at[side])
 
     load_forcing.start()
-    for side in order:
-        load_op(side).start()
-    load_classes.start()
+    load_op(order[0]).start()
 
     partners = (
         (row > 0, {"row": row - 1}), (row < row_count - 1, {"row": row + 1}),
@@ -83,7 +81,7 @@
         )
 
     twin_in, twin_out = 1 - core, core
-    shared = [(row >= 0, 0, twin_in, twin_out)]
+    shared = []
     for d in (0, 1):
         enters, leaves = has_col(d), gives_col(d)
         shared.append((leaves, 1 + 3 * d, twin_in, 3 - d))
@@ -96,7 +94,7 @@
             def _(slot=slot, in_side=in_side, out_side=out_side):
                 act(mat_copy(slot, in_side, out_side))
 
-    all_shared(lambda copy: copy.start())
+    mat_copy(0, twin_in, twin_out).start()
 
     def base_copy(slot, side):
         return remote(base.at[side], twin_base.at[slot], base_sem, (slot,), {"row": twin})
@@ -104,8 +102,9 @@
     load_forcing.wait()
     half[...] = source[...].astype(jnp.bfloat16)
 
-    def make_base(side):
+    def make_base(side, after=lambda: None):
         load_op(side).wait()
+        after()
         base[side] = dot(half[...], mat[side])
 
         @pl.when(side == twin_out)
@@ -232,14 +231,14 @@
     def twin_terms():
         def one(position, carry):
             d = jnp.where(position == 0, first, 1 - first)
+
+            @pl.when(has_col(d))
+            def _():
+                relay_copy(d).wait_recv()
+                add_terms(twin_col.at[d], 2 + d)
+
             cross_copy(d).wait_recv()
             add_terms(twin_row.at[d], 1 - core)
-
-            @pl.when(has_col(d))
-            def _():
-                relay_copy(d).wait_recv()
-                add_terms(twin_col.at[d], 2 + d)
-
             return carry
 
         lax.fori_loop(0, 2, one, 0)
@@ -248,7 +247,14 @@
         jnp.where(low_half, 0, 1) == core,
         jnp.logical_not(jnp.logical_or(has_row, has_col(first))),
     )
-    make_base(order[0])
+
+    def other_loads():
+        for side in order[1:]:
+            load_op(side).start()
+        load_classes.start()
+        all_shared(lambda copy: copy.start())
+
+    make_base(order[0], other_loads)
 
     @pl.when(early)
     def _():
@@ -308,7 +314,7 @@
             from_ref.at[side], to_ref.at[0, 0, :, where], out_sem.at[kind, side]
         )
 
-    for side in range(4):
+    for side in (2, 3, 0, 1):
         there, who = neighbours[side]
         rim_sent[side] = (acc[side] * 0.25).astype(jnp.bfloat16)
 
@@ -349,6 +355,7 @@
         out_copy(0, side).wait()
         out_copy(1, side).wait()
     coupling_copy.wait()
+    mat_copy(0, 0, 0).wait_send()
     all_shared(lambda copy: copy.wait_send())
     base_copy(0, 0).wait_send()
     for d in (0, 1):

time: 46.2 us -> 45.8 us (level)
  no operation moved by 1% of the time
where the time goes in v5:
time: 45.8 us; the launch traced here: 45.7 us
  Pallas kernels  42.4 us (93%)
  other arithmetic  2.6 us (6%)
  between operations  0.65 us (1%)
    pallas_call x1, Pallas kernels, local(): pl.pallas_call(functools.partial(kernel, row_count, col_count), out_shape...  42.4 us
    add x1, other arithmetic, local(): residual = forcing - preconditioned + coupling[:, :, None, :] * gap  2.6 us

profile of v5, /device:TPU:31, one launch (start us, length us, event | category | flops | bytes accessed | tf_op | source)
XLA Modules:
  0.0 45.7 jit_solution(8224962365988201623)
XLA Ops:
  0.6 0.0 copy-start
  0.6 42.4 %shard_map.59 = (f32[1,1,96,2048]{3,2,1,0:T(8,128)}, bf16[1,1,96,2048]{3,2,1,0:T(8,128)(2,1)}, f32[1,1,2048]{2,1,0:T(1,128)}) custom-call(f32[1,1,96,2048]{3,2,1,0:T(8,128)} %forcing.1, bf16[1,1,2048,2048]{3,2,1,0:T(8,128)(2,1)} %op.1, s32[1,1,2048]{2,1,0:T(1,128)} %material.1, f32[8]{0:T(128)} %stiffness.1), custom_call_target="tpu_custom_call" | custom-call | tf_op jit(solution)/shard_map/pallas_call | solution.py:388
  43.1 0.0 copy-done
  43.1 2.6 %multiply_add_fusion = (f32[1,1,96,2048]{3,2,1,0:T(8,128)}, f32[1,1,96,2048]{3,2,1,0:T(8,128)}) fusion(bf16[1,1,96,2048]{3,2,1,0:T(8,128)(2,1)} %get-tuple-element.7, f32[1,1,96,2048]{3,2,1,0:T(8,128)S(1)} %copy-done, f32[2048]{0:T(1024)} %bitcast.1, f32[1,1,96,2048]{3,2,1,0:T(8,128)} %get-tuple-element.5), kind=kLoop, calls=%fused_computation | loop fusion | flops 1179648 | bytes 3547136 | tf_op jit(solution)/shard_map/add | solution.py:434
Async XLA Ops:
  0.6 42.4 %copy-start = (f32[1,1,96,2048]{3,2,1,0:T(8,128)S(1)}, f32[1,1,96,2048]{3,2,1,0:T(8,128)}, u32[]{:S(2)}) copy-start(f32[1,1,96,2048]{3,2,1,0:T(8,128)} %forcing.1) | copy-start | bytes 2359300

commit v6 on v5

--- a/solution.py
+++ b/solution.py
@@ -381,7 +381,7 @@
     _, _, loads, order = forcing.shape
     width = order // 4
     side = (loads, width)
-    chunks = 2 if loads % 32 == 0 else 1
+    chunks = next(n for n in (3, 2, 1) if loads % (16 * n) == 0)
     any_spec = pl.BlockSpec(memory_space=pl.ANY)
     dma = pltpu.SemaphoreType.DMA
     f32, b16 = jnp.float32, jnp.bfloat16

time: 45.8 us -> 45.2 us (0.987)
  Pallas kernels: 42.4 us -> 41.7 us
    pallas_call x1, Pallas kernels: 42.4 us -> 41.7 us  [local(): pl.pallas_call(functools.partial(kernel, row_count, col_count), out_shape...]
where the time goes in v6:
time: 45.2 us; the launch traced here: 45 us
  Pallas kernels  41.7 us (92%)
  other arithmetic  2.6 us (6%)
  between operations  0.65 us (1%)
    pallas_call x1, Pallas kernels, local(): pl.pallas_call(functools.partial(kernel, row_count, col_count), out_shape...  41.7 us
    add x1, other arithmetic, local(): residual = forcing - preconditioned + coupling[:, :, None, :] * gap  2.6 us

profile of v6, /device:TPU:31, one launch (start us, length us, event | category | flops | bytes accessed | tf_op | source)
XLA Modules:
  0.0 45.0 jit_solution(13267121328408404460)
XLA Ops:
  0.6 0.0 copy-start
  0.6 41.7 %shard_map.59 = (f32[1,1,96,2048]{3,2,1,0:T(8,128)}, bf16[1,1,96,2048]{3,2,1,0:T(8,128)(2,1)}, f32[1,1,2048]{2,1,0:T(1,128)}) custom-call(f32[1,1,96,2048]{3,2,1,0:T(8,128)} %forcing.1, bf16[1,1,2048,2048]{3,2,1,0:T(8,128)(2,1)} %op.1, s32[1,1,2048]{2,1,0:T(1,128)} %material.1, f32[8]{0:T(128)} %stiffness.1), custom_call_target="tpu_custom_call" | custom-call | tf_op jit(solution)/shard_map/pallas_call | solution.py:388
  42.4 0.0 copy-done
  42.4 2.6 %multiply_add_fusion = (f32[1,1,96,2048]{3,2,1,0:T(8,128)}, f32[1,1,96,2048]{3,2,1,0:T(8,128)}) fusion(bf16[1,1,96,2048]{3,2,1,0:T(8,128)(2,1)} %get-tuple-element.7, f32[1,1,96,2048]{3,2,1,0:T(8,128)S(1)} %copy-done, f32[2048]{0:T(1024)} %bitcast.1, f32[1,1,96,2048]{3,2,1,0:T(8,128)} %get-tuple-element.5), kind=kLoop, calls=%fused_computation | loop fusion | flops 1179648 | bytes 3547136 | tf_op jit(solution)/shard_map/add | solution.py:434
Async XLA Ops:
  0.6 41.8 %copy-start = (f32[1,1,96,2048]{3,2,1,0:T(8,128)S(1)}, f32[1,1,96,2048]{3,2,1,0:T(8,128)}, u32[]{:S(2)}) copy-start(f32[1,1,96,2048]{3,2,1,0:T(8,128)} %forcing.1) | copy-start | bytes 2359300
